TPU v7x, 32 devices: a whole 2x2x4 slice. The times are simulated.
32 devices in a mesh: wide: 16 (over z, y, x), narrow: 2 (over core).
Axes of the slice: x: 2, y: 2, z: 4, core: 2. Of those that a mesh axis runs over, the one named last changes fastest.
Arguments:
- right_side: float32 [256, 32, 128], P('wide', 'narrow'), may hold values from -8 to 8
- labels: int32 [32, 4, 16], P('wide', 'narrow'), may hold values from 0 to 15
- material_table: float32 [16], replicated, may hold values from 0.1 to 10
- robin_table: float32 [8], replicated, may hold values from 0.5 to 8
- robin_index: int32 [16, 2, 2], P('wide', 'narrow'), may hold values from 0 to 7
- coarse_rows: float32 [32, 32], P(('wide', 'narrow')), may hold values from -0.005859375 to 0.005859375
Outputs:
- solution: bfloat16 [256, 32, 128], P('wide', 'narrow')
- residual: bfloat16 [256, 32, 128], P('wide', 'narrow')
All inputs are finite; a program needn't handle non-finite values.
Results may differ from a plain program's by a relative error of at most 0.0015.
Values sent between devices are 32-bit elements; how exact they have to be, the bound alone decides.
A program may use at most 64 MiB of HBM per device.

v0:
```python
import jax
import jax.numpy as jnp
from jax import lax
from jax.sharding import PartitionSpec as P

BLOCK = 8
SWEEPS = 4
ITERS = 2


reaction = 1.0


def extended(cells, sides, width):
    for axis, dim in sides:
        count = lax.axis_size(axis)
        ends = count - 1
        head = lax.slice_in_dim(cells, 0, width, axis=dim)
        tail = lax.slice_in_dim(cells, cells.shape[dim] - width, cells.shape[dim], axis=dim)
        cells = jnp.concatenate(
            [
                lax.ppermute(tail, axis, [(i, (i + 1) % count) for i in range(ends)]),
                cells,
                lax.ppermute(head, axis, [((i + 1) % count, i) for i in range(ends)]),
            ],
            axis=dim,
        )
    return cells


def shifted(array, axis, by):
    peers = lax.axis_size(axis)
    pairs = [(i, i + by) for i in range(peers) if 0 <= i + by < peers]
    return lax.ppermute(array, axis, pairs)


def spread_cells(blocks):
    size_a, size_b, size_c = blocks.shape
    grown_up = jnp.broadcast_to(
        blocks[:, None, :, None, :, None], (size_a, BLOCK, size_b, BLOCK, size_c, BLOCK)
    )
    return grown_up.reshape(size_a * BLOCK, size_b * BLOCK, size_c * BLOCK)


def spread_face(blocks):
    size_a, size_b = blocks.shape
    grown_up = jnp.broadcast_to(blocks[:, None, :, None], (size_a, BLOCK, size_b, BLOCK))
    return grown_up.reshape(size_a * BLOCK, size_b * BLOCK)


def face_conduct(kappa, west_k, east_k, south_k, north_k):
    west_v = jnp.concatenate([west_k[None], kappa[:-1]], 0)
    east_v = jnp.concatenate([kappa[1:], east_k[None]], 0)
    south_v = jnp.concatenate([south_k[:, None], kappa[:, :-1]], 1)
    north_v = jnp.concatenate([kappa[:, 1:], north_k[:, None]], 1)
    below_v = jnp.concatenate([kappa[:, :, :1], kappa[:, :, :-1]], 2)
    above_v = jnp.concatenate([kappa[:, :, 1:], kappa[:, :, -1:]], 2)
    return (
        0.5 * (kappa + west_v),
        0.5 * (kappa + east_v),
        0.5 * (kappa + south_v),
        0.5 * (kappa + north_v),
        0.5 * (kappa + below_v),
        0.5 * (kappa + above_v),
    )


def neighbour_sum(field_now, conduct, borders):
    zero_layer = jnp.zeros_like(field_now[:, :, :1])
    coupled = conduct[0] * jnp.concatenate([borders[0][None], field_now[:-1]], 0)
    coupled = coupled + conduct[1] * jnp.concatenate([field_now[1:], borders[1][None]], 0)
    coupled = coupled + conduct[2] * jnp.concatenate([borders[2][:, None], field_now[:, :-1]], 1)
    coupled = coupled + conduct[3] * jnp.concatenate([field_now[:, 1:], borders[3][:, None]], 1)
    coupled = coupled + conduct[4] * jnp.concatenate([zero_layer, field_now[:, :, :-1]], 2)
    return coupled + conduct[5] * jnp.concatenate([field_now[:, :, 1:], zero_layer], 2)


def side_marks(shape):
    index_x = lax.broadcasted_iota(jnp.int32, (shape[0], shape[1], 1), 0)
    index_y = lax.broadcasted_iota(jnp.int32, (shape[0], shape[1], 1), 1)
    return (
        (index_x == 0).astype(jnp.float32),
        (index_x == shape[0] - 1).astype(jnp.float32),
        (index_y == 0).astype(jnp.float32),
        (index_y == shape[1] - 1).astype(jnp.float32),
    )


def assemble_local(material):
    kappa_blocks, west_b, east_b, south_b, north_b, inside, robin_pair = material
    kappa = spread_cells(kappa_blocks)
    sides = (spread_face(west_b), spread_face(east_b), spread_face(south_b), spread_face(north_b))
    owned = (kappa[0], kappa[-1], kappa[:, 0], kappa[:, -1])
    chosen = [jnp.where(inside[side] > 0, sides[side], owned[side]) for side in range(4)]
    conduct = face_conduct(kappa, chosen[0], chosen[1], chosen[2], chosen[3])
    conduct_sum = conduct[0] + conduct[1] + conduct[2] + conduct[3] + conduct[4] + conduct[5]
    marks = side_marks(kappa.shape)
    robin_term = robin_pair[0] * (inside[0] * marks[0] + inside[1] * marks[1]) + robin_pair[1] * (
        inside[2] * marks[2] + inside[3] * marks[3]
    )
    parity = (
        lax.broadcasted_iota(jnp.int32, kappa.shape, 0)
        + lax.broadcasted_iota(jnp.int32, kappa.shape, 1)
        + lax.broadcasted_iota(jnp.int32, kappa.shape, 2)
    ) % 2
    return (conduct, conduct_sum, robin_term, parity)


def robin_source(traces, shape):
    marks = side_marks(shape)
    return (
        marks[0] * traces[0][None]
        + marks[1] * traces[1][None]
        + marks[2] * traces[2][:, None]
        + marks[3] * traces[3][:, None]
    )


def relax(field_now, source, conduct, diagonal, parity):
    blank_x = jnp.zeros_like(field_now[0])
    blank_y = jnp.zeros_like(field_now[:, 0])
    blanks = (blank_x, blank_x, blank_y, blank_y)
    for sweep_at in range(SWEEPS):
        for colour in range(2):
            update = (source + neighbour_sum(field_now, conduct, blanks)) / diagonal
            field_now = jnp.where(parity == colour, update, field_now)
    return field_now


def misfit(field_now, source_part, conduct, conduct_sum, borders):
    return (
        source_part
        - (reaction + conduct_sum) * field_now
        + neighbour_sum(field_now, conduct, borders)
    )


def coarse_weights(extent_x, extent_y):
    along_x = (jnp.arange(extent_x, dtype=jnp.float32) + 0.5) / extent_x
    along_y = (jnp.arange(extent_y, dtype=jnp.float32) + 0.5) / extent_y
    return (
        (1.0 - along_x)[:, None] * (1.0 - along_y)[None, :],
        along_x[:, None] * (1.0 - along_y)[None, :],
        (1.0 - along_x)[:, None] * along_y[None, :],
        along_x[:, None] * along_y[None, :],
    )


def restrict(leftover):
    column_sum = jnp.sum(leftover, axis=2)
    weights = coarse_weights(leftover.shape[0], leftover.shape[1])
    return jnp.stack([jnp.sum(weights[corner] * column_sum) for corner in range(4)])


def interpolate(corners, extent_x, extent_y):
    weights = coarse_weights(extent_x, extent_y)
    return (
        corners[0, 0] * weights[0]
        + corners[1, 0] * weights[1]
        + corners[0, 1] * weights[2]
        + corners[1, 1] * weights[3]
    )


def robin_traces(field_now, borders, conduct, inside, robin_pair):
    return (
        inside[0] * (conduct[0][0] * borders[0] + robin_pair[0] * field_now[0]),
        inside[1] * (conduct[1][-1] * borders[1] + robin_pair[0] * field_now[-1]),
        inside[2] * (conduct[2][:, 0] * borders[2] + robin_pair[1] * field_now[:, 0]),
        inside[3] * (conduct[3][:, -1] * borders[3] + robin_pair[1] * field_now[:, -1]),
    )


def combine_partials(stacked):
    from_west = jnp.pad(stacked[:-1, :, 1], ((1, 0), (0, 0)))
    from_south = jnp.pad(stacked[:, :-1, 2], ((0, 0), (1, 0)))
    from_corner = jnp.pad(stacked[:-1, :-1, 3], ((1, 0), (1, 0)))
    return stacked[:, :, 0] + from_west + from_south + from_corner


def table_lookup(keys, table):
    entries = jnp.arange(table.shape[0], dtype=jnp.int32)
    return jnp.sum(jnp.where(keys[..., None] == entries, table, 0.0), -1)


def face_rows(widened):
    return (widened[0, 1:-1], widened[-1, 1:-1], widened[1:-1, 0], widened[1:-1, -1])


def body(right_side, labels, material_table, robin_table, robin_index, coarse_rows):
    wide_at = lax.axis_index("wide")
    narrow_at = lax.axis_index("narrow")
    wide_count = lax.axis_size("wide")
    narrow_count = lax.axis_size("narrow")
    extent_x, extent_y = (right_side.shape[0], right_side.shape[1])
    label_pad = extended(labels, (("wide", 0), ("narrow", 1)), 1)
    kappa_pad = table_lookup(label_pad, material_table)
    inside = jnp.stack(
        [wide_at > 0, wide_at < wide_count - 1, narrow_at > 0, narrow_at < narrow_count - 1]
    ).astype(jnp.float32)
    robin_pair = table_lookup(robin_index[0, 0], robin_table)
    material = (
        kappa_pad[1:-1, 1:-1],
        kappa_pad[0, 1:-1],
        kappa_pad[-1, 1:-1],
        kappa_pad[1:-1, 0],
        kappa_pad[1:-1, -1],
        inside,
        robin_pair,
    )
    conduct, conduct_sum, robin_term, parity = assemble_local(material)
    diagonal = reaction + conduct_sum + robin_term
    solution_now = jnp.zeros_like(right_side)
    traces = (
        jnp.zeros_like(right_side[0]),
        jnp.zeros_like(right_side[0]),
        jnp.zeros_like(right_side[:, 0]),
        jnp.zeros_like(right_side[:, 0]),
    )
    for outer in range(ITERS):
        source = right_side + robin_source(traces, right_side.shape)
        solution_now = relax(solution_now, source, conduct, diagonal, parity)
        widened = extended(solution_now, (("wide", 0), ("narrow", 1)), 1)
        borders = face_rows(widened)
        partial_value = restrict(misfit(solution_now, right_side, conduct, conduct_sum, borders))
        every = lax.all_gather(partial_value[None], ("wide", "narrow"), axis=0, tiled=True)
        coarse_vec = combine_partials(every.reshape(wide_count, narrow_count, 4)).reshape(-1)
        coarse_own = jnp.dot(
            coarse_rows,
            coarse_vec,
            precision=lax.Precision.HIGHEST,
            preferred_element_type=jnp.float32,
        )
        east_value = shifted(coarse_own, "wide", -1)
        column_pair = jnp.stack([coarse_own[0], east_value[0]])
        north_pair = shifted(column_pair, "narrow", -1)
        corners = jnp.stack(
            [jnp.stack([column_pair[0], north_pair[0]]), jnp.stack([column_pair[1], north_pair[1]])]
        )
        solution_now = solution_now + interpolate(corners, extent_x, extent_y)[:, :, None]
        widened = extended(solution_now, (("wide", 0), ("narrow", 1)), 1)
        borders = face_rows(widened)
        if outer + 1 < ITERS:
            traces = robin_traces(solution_now, borders, conduct, inside, robin_pair)
    leftover = misfit(solution_now, right_side, conduct, conduct_sum, borders)
    return (solution_now.astype(jnp.bfloat16), leftover.astype(jnp.bfloat16))


def solution(mesh):
    placed = (
        P("wide", "narrow", None),
        P("wide", "narrow", None),
        P(),
        P(),
        P("wide", "narrow", None),
        P(("wide", "narrow"), None),
    )
    return jax.shard_map(
        body,
        mesh=mesh,
        in_specs=placed,
        out_specs=(P("wide", "narrow", None), P("wide", "narrow", None)),
        check_vma=False,
    )
```

profile of v0, /device:TPU:0, one launch (start us, length us, event | category | flops | bytes accessed | tf_op | source)
XLA Modules:
  0.0 226.3 jit_solution(12275487693717933623)
XLA Ops:
  1.3 4.9 %collective-permute-start = (s32[1,2,16]{2,1,0:T(2,128)S(1)}, s32[1,2,16]{2,1,0:T(2,128)S(1)}, u32[]{:S(2)}, u32[]{:S(2)}) collective-permute-start(s32[1,2,16]{2,1,0:T(2,128)S(1)} %get-tuple-element.164), channel_id=1, source_target_pairs={{0,2},{2,4},{4,6},{6,8},{8,10},{10,12},{12,14},{14,16},{16,18},{18... | collective-permute-start | bytes 392 | tf_op jit(solution)/shard_map/ppermute | solution.py:22
  11.1 3.9 %add_multiply_fusion.1 = (f32[16]{0:T(128)S(1)}, f32[16]{0:T(128)S(1)}) fusion(f32[]{:T(128)} %bitcast.11, f32[]{:T(128)} %bitcast.8, f32[]{:T(128)} %bitcast.16, f32[]{:T(128)} %bitcast.6, f32[]{:T(128)} %bitcast.4, f32[]{:T(128)} %bitcast.15), kind=kLoop, calls=%fused_computation.171 | loop fusion | flops 160 | bytes 152 | tf_op jit(solution)/shard_map/mul | solution.py:98
  19.8 1.7 collective-permute-done.3
  27.8 4.4 %collective-permute-start.4 = (f32[1,16,128]{2,1,0:T(8,128)S(1)}, f32[1,16,128]{2,1,0:T(8,128)S(1)}, u32[]{:S(2)}, u32[]{:S(2)}) collective-permute-start(f32[1,16,128]{2,1,0:T(8,128)S(1)} %get-tuple-element.102), channel_id=1, source_target_pairs={{0,2},{2,4},{4,6},{6,8},{8,10},{10,12},{12,14},{14,16},{16,18},{18... | collective-permute-start | bytes 24584 | tf_op jit(solution)/shard_map/ppermute | solution.py:22
  33.5 4.6 %collective-permute-done.5 = f32[1,16,128]{2,1,0:T(8,128)S(1)} collective-permute-done((f32[1,16,128]{2,1,0:T(8,128)S(1)}, f32[1,16,128]{2,1,0:T(8,128)S(1)}, u32[]{:S(2)}, u32[]{:S(2)}) %collective-permute-start.5) | collective-permute-done | bytes 8224 | tf_op jit(solution)/shard_map/ppermute | solution.py:24
  40.7 1.7 collective-permute-done.7
  43.5 2.6 %maximum_dynamic-update-slice_fusion = f32[128]{0:T(128)S(1)} fusion(f32[128]{0:T(128)S(1)} %broadcast.596.clone, u32[]{:T(128)S(6)} %multiply.33, f32[1]{0:T(128)} %bitcast.20, f32[1]{0:T(128)} %bitcast.19, f32[1]{0:T(128)} %bitcast.18, f32[1]{0:T(128)} %bitcast.17), kind=kLoop, calls=%fused_computation.158 | loop fusion | flops 12 | bytes 532
  46.0 43.6 %all-reduce.102 = f32[128]{0:T(128)S(1)} all-reduce(f32[128]{0:T(128)S(1)} %maximum_dynamic-update-slice_fusion), channel_id=2, replica_groups=mesh['wide'=16,'narrow'=2] {'wide','narrow'}, use_global_device_ids=true, to_apply=%add.102 | all-reduce | flops 128 | bytes 1024
  92.7 4.7 %collective-permute-done.8 = f32[1]{0:T(128)} collective-permute-done((f32[1]{0:T(128)}, f32[1]{0:T(128)}, u32[]{:S(2)}, u32[]{:S(2)}) %collective-permute-start.8) | collective-permute-done | bytes 36 | tf_op jit(solution)/shard_map/ppermute | solution.py:34
  100.0 1.8 collective-permute-done.9
  106.2 2.5 %fusion.30 = f32[16,16]{1,0:T(8,128)S(1)} fusion(f32[]{:T(128)} %bitcast.30, f32[]{:T(128)} %bitcast.29, f32[]{:T(128)} %bitcast.28, f32[]{:T(128)} %bitcast.26, f32[16]{0:T(128)S(1)} %get-tuple-element.185, f32[16]{0:T(128)S(1)} %get-tuple-element.186), kind=kLoop, calls=%fused_computation.109 | loop fusion | flops 2816 | bytes 1168 | tf_op jit(solution)/shard_map/add | solution.py:158
  108.9 4.8 %collective-permute-start.10 = (f32[1,16,128]{2,1,0:T(8,128)S(1)}, f32[1,16,128]{2,1,0:T(8,128)S(1)}, u32[]{:S(2)}, u32[]{:S(2)}) collective-permute-start(f32[1,16,128]{2,1,0:T(8,128)S(1)} %slice.830), channel_id=1, source_target_pairs={{0,2},{2,4},{4,6},{6,8},{8,10},{10,12},{12,14},{14,16},{16,18},{18... | collective-permute-start | bytes 24584 | tf_op jit(solution)/shard_map/ppermute | solution.py:22
  117.6 4.5 %collective-permute-done.11 = f32[1,16,128]{2,1,0:T(8,128)S(1)} collective-permute-done((f32[1,16,128]{2,1,0:T(8,128)S(1)}, f32[1,16,128]{2,1,0:T(8,128)S(1)}, u32[]{:S(2)}, u32[]{:S(2)}) %collective-permute-start.11) | collective-permute-done | bytes 8224 | tf_op jit(solution)/shard_map/ppermute | solution.py:24
  126.5 2.0 fusion.49
  131.8 4.8 %collective-permute-start.14 = (f32[1,16,128]{2,1,0:T(8,128)S(1)}, f32[1,16,128]{2,1,0:T(8,128)S(1)}, u32[]{:S(2)}, u32[]{:S(2)}) collective-permute-start(f32[1,16,128]{2,1,0:T(8,128)S(1)} %get-tuple-element.42), channel_id=1, source_target_pairs={{0,2},{2,4},{4,6},{6,8},{8,10},{10,12},{12,14},{14,16},{16,18},{18... | collective-permute-start | bytes 24584 | tf_op jit(solution)/shard_map/ppermute | solution.py:22
  138.0 4.2 %collective-permute-done.15 = f32[1,16,128]{2,1,0:T(8,128)S(1)} collective-permute-done((f32[1,16,128]{2,1,0:T(8,128)S(1)}, f32[1,16,128]{2,1,0:T(8,128)S(1)}, u32[]{:S(2)}, u32[]{:S(2)}) %collective-permute-start.15) | collective-permute-done | bytes 8224 | tf_op jit(solution)/shard_map/ppermute | solution.py:24
  144.9 1.7 collective-permute-done.17
  147.6 2.7 %maximum_dynamic-update-slice_fusion.1 = f32[128]{0:T(128)S(1)} fusion(f32[128]{0:T(128)S(1)} %broadcast.596, u32[]{:T(128)S(6)} %multiply.33, f32[1]{0:T(128)} %bitcast.38, f32[1]{0:T(128)} %bitcast.37, f32[1]{0:T(128)} %bitcast.36, f32[1]{0:T(128)} %bitcast.35), kind=kLoop, calls=%fused_computation.162 | loop fusion | flops 12 | bytes 532
  150.3 40.3 %all-reduce.103 = f32[128]{0:T(128)S(1)} all-reduce(f32[128]{0:T(128)S(1)} %maximum_dynamic-update-slice_fusion.1), channel_id=3, replica_groups=mesh['wide'=16,'narrow'=2] {'wide','narrow'}, use_global_device_ids=true, to_apply=%add.103 | all-reduce | flops 128 | bytes 1024
  193.8 4.5 %collective-permute-done.18 = f32[1]{0:T(128)} collective-permute-done((f32[1]{0:T(128)}, f32[1]{0:T(128)}, u32[]{:S(2)}, u32[]{:S(2)}) %collective-permute-start.18) | collective-permute-done | bytes 36 | tf_op jit(solution)/shard_map/ppermute | solution.py:34
  201.0 1.8 collective-permute-done.19
  207.3 2.7 %fusion.34 = f32[16,16]{1,0:T(8,128)S(1)} fusion(f32[]{:T(128)} %bitcast.47, f32[]{:T(128)} %bitcast.46, f32[]{:T(128)} %bitcast.45, f32[]{:T(128)} %bitcast.43, f32[16]{0:T(128)S(1)} %get-tuple-element.185, f32[16]{0:T(128)S(1)} %get-tuple-element.186), kind=kLoop, calls=%fused_computation.113 | loop fusion | flops 2816 | bytes 1168 | tf_op jit(solution)/shard_map/add | solution.py:158
  210.8 4.8 %collective-permute-start.20 = (f32[1,16,128]{2,1,0:T(8,128)S(1)}, f32[1,16,128]{2,1,0:T(8,128)S(1)}, u32[]{:S(2)}, u32[]{:S(2)}) collective-permute-start(f32[1,16,128]{2,1,0:T(8,128)S(1)} %get-tuple-element.34), channel_id=1, source_target_pairs={{0,2},{2,4},{4,6},{6,8},{8,10},{10,12},{12,14},{14,16},{16,18},{18... | collective-permute-start | bytes 24584 | tf_op jit(solution)/shard_map/ppermute | solution.py:22
  217.0 4.2 %collective-permute-done.21 = f32[1,16,128]{2,1,0:T(8,128)S(1)} collective-permute-done((f32[1,16,128]{2,1,0:T(8,128)S(1)}, f32[1,16,128]{2,1,0:T(8,128)S(1)}, u32[]{:S(2)}, u32[]{:S(2)}) %collective-permute-start.21) | collective-permute-done | bytes 8224 | tf_op jit(solution)/shard_map/ppermute | solution.py:24
  (196 shorter events, 62.8 us)
Async XLA Ops:
  1.3 15.0 %collective-permute-start = (s32[1,2,16]{2,1,0:T(2,128)S(1)}, s32[1,2,16]{2,1,0:T(2,128)S(1)}, u32[]{:S(2)}, u32[]{:S(2)}) collective-permute-start(s32[1,2,16]{2,1,0:T(2,128)S(1)} %get-tuple-element.164), channel_id=1, source_target_pairs={{0,2},{2,4},{4,6},{6,8},{8,10},{10,12},{12,14},{14,16},{16,18},{18... | collective-permute-start | bytes 392 | tf_op jit(solution)/shard_map/ppermute | solution.py:22
  6.2 10.8 %collective-permute-start.1 = (s32[1,2,16]{2,1,0:T(2,128)S(1)}, s32[1,2,16]{2,1,0:T(2,128)S(1)}, u32[]{:S(2)}, u32[]{:S(2)}) collective-permute-start(s32[1,2,16]{2,1,0:T(2,128)S(1)} %get-tuple-element.163), channel_id=1, source_target_pairs={{2,0},{4,2},{6,4},{8,6},{10,8},{12,10},{14,12},{16,14},{18,16},{20... | collective-permute-start | bytes 392 | tf_op jit(solution)/shard_map/ppermute | solution.py:24
  17.0 2.8 %collective-permute-start.2 = (s32[4,1,16]{2,1,0:T(1,128)S(1)}, s32[4,1,16]{2,1,0:T(1,128)S(1)}, u32[]{:S(2)}, u32[]{:S(2)}) collective-permute-start(s32[4,1,16]{2,1,0:T(1,128)S(1)} %get-tuple-element.161), channel_id=1, source_target_pairs={{0,1},{2,3},{4,5},{6,7},{8,9},{10,11},{12,13},{14,15},{16,17},{18,... | collective-permute-start | bytes 776 | tf_op jit(solution)/shard_map/ppermute | solution.py:22
  18.5 3.1 %collective-permute-start.3 = (s32[4,1,16]{2,1,0:T(1,128)S(1)}, s32[4,1,16]{2,1,0:T(1,128)S(1)}, u32[]{:S(2)}, u32[]{:S(2)}) collective-permute-start(s32[4,1,16]{2,1,0:T(1,128)S(1)} %get-tuple-element.162), channel_id=1, source_target_pairs={{1,0},{3,2},{5,4},{7,6},{9,8},{11,10},{13,12},{15,14},{17,16},{19,... | collective-permute-start | bytes 776 | tf_op jit(solution)/shard_map/ppermute | solution.py:24
  27.8 5.7 %collective-permute-start.4 = (f32[1,16,128]{2,1,0:T(8,128)S(1)}, f32[1,16,128]{2,1,0:T(8,128)S(1)}, u32[]{:S(2)}, u32[]{:S(2)}) collective-permute-start(f32[1,16,128]{2,1,0:T(8,128)S(1)} %get-tuple-element.102), channel_id=1, source_target_pairs={{0,2},{2,4},{4,6},{6,8},{8,10},{10,12},{12,14},{14,16},{16,18},{18... | collective-permute-start | bytes 24584 | tf_op jit(solution)/shard_map/ppermute | solution.py:22
  32.1 5.9 %collective-permute-start.5 = (f32[1,16,128]{2,1,0:T(8,128)S(1)}, f32[1,16,128]{2,1,0:T(8,128)S(1)}, u32[]{:S(2)}, u32[]{:S(2)}) collective-permute-start(f32[1,16,128]{2,1,0:T(8,128)S(1)} %get-tuple-element.101), channel_id=1, source_target_pairs={{2,0},{4,2},{6,4},{8,6},{10,8},{12,10},{14,12},{16,14},{18,16},{20... | collective-permute-start | bytes 24584 | tf_op jit(solution)/shard_map/ppermute | solution.py:24
  38.1 2.6 %collective-permute-start.6 = (f32[18,1,128]{2,1,0:T(1,128)S(1)}, f32[18,1,128]{2,1,0:T(1,128)S(1)}, u32[]{:S(2)}, u32[]{:S(2)}) collective-permute-start(f32[18,1,128]{2,1,0:T(1,128)S(1)} %get-tuple-element.26), channel_id=1, source_target_pairs={{0,1},{2,3},{4,5},{6,7},{8,9},{10,11},{12,13},{14,15},{16,17},{18,... | collective-permute-start | bytes 27656 | tf_op jit(solution)/shard_map/ppermute | solution.py:22
  39.4 3.1 %collective-permute-start.7 = (f32[18,1,128]{2,1,0:T(1,128)S(1)}, f32[18,1,128]{2,1,0:T(1,128)S(1)}, u32[]{:S(2)}, u32[]{:S(2)}) collective-permute-start(f32[18,1,128]{2,1,0:T(1,128)S(1)} %get-tuple-element.25), channel_id=1, source_target_pairs={{1,0},{3,2},{5,4},{7,6},{9,8},{11,10},{13,12},{15,14},{17,16},{19,... | collective-permute-start | bytes 27656 | tf_op jit(solution)/shard_map/ppermute | solution.py:24
  91.4 6.0 %collective-permute-start.8 = (f32[1]{0:T(128)}, f32[1]{0:T(128)}, u32[]{:S(2)}, u32[]{:S(2)}) collective-permute-start(f32[1]{0:T(128)} %bitcast.24), channel_id=1, source_target_pairs={{2,0},{4,2},{6,4},{8,6},{10,8},{12,10},{14,12},{16,14},{18,16},{20... | collective-permute-start | bytes 20 | tf_op jit(solution)/shard_map/ppermute | solution.py:34
  98.7 3.0 %collective-permute-start.9 = (f32[2]{0:T(128)S(1)}, f32[2]{0:T(128)S(1)}, u32[]{:S(2)}, u32[]{:S(2)}) collective-permute-start(f32[2]{0:T(128)S(1)} %pad_maximum_fusion.12), channel_id=1, source_target_pairs={{1,0},{3,2},{5,4},{7,6},{9,8},{11,10},{13,12},{15,14},{17,16},{19,... | collective-permute-start | bytes 32 | tf_op jit(solution)/shard_map/ppermute | solution.py:34
  108.9 6.2 %collective-permute-start.10 = (f32[1,16,128]{2,1,0:T(8,128)S(1)}, f32[1,16,128]{2,1,0:T(8,128)S(1)}, u32[]{:S(2)}, u32[]{:S(2)}) collective-permute-start(f32[1,16,128]{2,1,0:T(8,128)S(1)} %slice.830), channel_id=1, source_target_pairs={{0,2},{2,4},{4,6},{6,8},{8,10},{10,12},{12,14},{14,16},{16,18},{18... | collective-permute-start | bytes 24584 | tf_op jit(solution)/shard_map/ppermute | solution.py:22
  116.3 5.8 %collective-permute-start.11 = (f32[1,16,128]{2,1,0:T(8,128)S(1)}, f32[1,16,128]{2,1,0:T(8,128)S(1)}, u32[]{:S(2)}, u32[]{:S(2)}) collective-permute-start(f32[1,16,128]{2,1,0:T(8,128)S(1)} %get-tuple-element.86), channel_id=1, source_target_pairs={{2,0},{4,2},{6,4},{8,6},{10,8},{12,10},{14,12},{16,14},{18,16},{20... | collective-permute-start | bytes 24584 | tf_op jit(solution)/shard_map/ppermute | solution.py:24
  122.1 3.8 %collective-permute-start.12 = (f32[18,1,128]{2,1,0:T(1,128)S(1)}, f32[18,1,128]{2,1,0:T(1,128)S(1)}, u32[]{:S(2)}, u32[]{:S(2)}) collective-permute-start(f32[18,1,128]{2,1,0:T(1,128)S(1)} %get-tuple-element.23), channel_id=1, source_target_pairs={{0,1},{2,3},{4,5},{6,7},{8,9},{10,11},{12,13},{14,15},{16,17},{18,... | collective-permute-start | bytes 27656 | tf_op jit(solution)/shard_map/ppermute | solution.py:22
  123.4 3.1 %collective-permute-start.13 = (f32[18,1,128]{2,1,0:T(1,128)S(1)}, f32[18,1,128]{2,1,0:T(1,128)S(1)}, u32[]{:S(2)}, u32[]{:S(2)}) collective-permute-start(f32[18,1,128]{2,1,0:T(1,128)S(1)} %get-tuple-element.24), channel_id=1, source_target_pairs={{1,0},{3,2},{5,4},{7,6},{9,8},{11,10},{13,12},{15,14},{17,16},{19,... | collective-permute-start | bytes 27656 | tf_op jit(solution)/shard_map/ppermute | solution.py:24
  131.8 6.2 %collective-permute-start.14 = (f32[1,16,128]{2,1,0:T(8,128)S(1)}, f32[1,16,128]{2,1,0:T(8,128)S(1)}, u32[]{:S(2)}, u32[]{:S(2)}) collective-permute-start(f32[1,16,128]{2,1,0:T(8,128)S(1)} %get-tuple-element.42), channel_id=1, source_target_pairs={{0,2},{2,4},{4,6},{6,8},{8,10},{10,12},{12,14},{14,16},{16,18},{18... | collective-permute-start | bytes 24584 | tf_op jit(solution)/shard_map/ppermute | solution.py:22
  136.7 5.5 %collective-permute-start.15 = (f32[1,16,128]{2,1,0:T(8,128)S(1)}, f32[1,16,128]{2,1,0:T(8,128)S(1)}, u32[]{:S(2)}, u32[]{:S(2)}) collective-permute-start(f32[1,16,128]{2,1,0:T(8,128)S(1)} %get-tuple-element.41), channel_id=1, source_target_pairs={{2,0},{4,2},{6,4},{8,6},{10,8},{12,10},{14,12},{16,14},{18,16},{20... | collective-permute-start | bytes 24584 | tf_op jit(solution)/shard_map/ppermute | solution.py:24
  142.2 2.6 %collective-permute-start.16 = (f32[18,1,128]{2,1,0:T(1,128)S(1)}, f32[18,1,128]{2,1,0:T(1,128)S(1)}, u32[]{:S(2)}, u32[]{:S(2)}) collective-permute-start(f32[18,1,128]{2,1,0:T(1,128)S(1)} %get-tuple-element.22), channel_id=1, source_target_pairs={{0,1},{2,3},{4,5},{6,7},{8,9},{10,11},{12,13},{14,15},{16,17},{18,... | collective-permute-start | bytes 27656 | tf_op jit(solution)/shard_map/ppermute | solution.py:22
  143.5 3.1 %collective-permute-start.17 = (f32[18,1,128]{2,1,0:T(1,128)S(1)}, f32[18,1,128]{2,1,0:T(1,128)S(1)}, u32[]{:S(2)}, u32[]{:S(2)}) collective-permute-start(f32[18,1,128]{2,1,0:T(1,128)S(1)} %get-tuple-element.21), channel_id=1, source_target_pairs={{1,0},{3,2},{5,4},{7,6},{9,8},{11,10},{13,12},{15,14},{17,16},{19,... | collective-permute-start | bytes 27656 | tf_op jit(solution)/shard_map/ppermute | solution.py:24
  192.5 5.8 %collective-permute-start.18 = (f32[1]{0:T(128)}, f32[1]{0:T(128)}, u32[]{:S(2)}, u32[]{:S(2)}) collective-permute-start(f32[1]{0:T(128)} %bitcast.41), channel_id=1, source_target_pairs={{2,0},{4,2},{6,4},{8,6},{10,8},{12,10},{14,12},{16,14},{18,16},{20... | collective-permute-start | bytes 20 | tf_op jit(solution)/shard_map/ppermute | solution.py:34
  199.7 3.0 %collective-permute-start.19 = (f32[2]{0:T(128)S(1)}, f32[2]{0:T(128)S(1)}, u32[]{:S(2)}, u32[]{:S(2)}) collective-permute-start(f32[2]{0:T(128)S(1)} %pad_maximum_fusion.13), channel_id=1, source_target_pairs={{1,0},{3,2},{5,4},{7,6},{9,8},{11,10},{13,12},{15,14},{17,16},{19,... | collective-permute-start | bytes 32 | tf_op jit(solution)/shard_map/ppermute | solution.py:34
  210.8 6.2 %collective-permute-start.20 = (f32[1,16,128]{2,1,0:T(8,128)S(1)}, f32[1,16,128]{2,1,0:T(8,128)S(1)}, u32[]{:S(2)}, u32[]{:S(2)}) collective-permute-start(f32[1,16,128]{2,1,0:T(8,128)S(1)} %get-tuple-element.34), channel_id=1, source_target_pairs={{0,2},{2,4},{4,6},{6,8},{8,10},{10,12},{12,14},{14,16},{16,18},{18... | collective-permute-start | bytes 24584 | tf_op jit(solution)/shard_map/ppermute | solution.py:22
  215.6 5.5 %collective-permute-start.21 = (f32[1,16,128]{2,1,0:T(8,128)S(1)}, f32[1,16,128]{2,1,0:T(8,128)S(1)}, u32[]{:S(2)}, u32[]{:S(2)}) collective-permute-start(f32[1,16,128]{2,1,0:T(8,128)S(1)} %get-tuple-element.33), channel_id=1, source_target_pairs={{2,0},{4,2},{6,4},{8,6},{10,8},{12,10},{14,12},{16,14},{18,16},{20... | collective-permute-start | bytes 24584 | tf_op jit(solution)/shard_map/ppermute | solution.py:24
  221.2 2.6 %collective-permute-start.22 = (f32[18,1,128]{2,1,0:T(1,128)S(1)}, f32[18,1,128]{2,1,0:T(1,128)S(1)}, u32[]{:S(2)}, u32[]{:S(2)}) collective-permute-start(f32[18,1,128]{2,1,0:T(1,128)S(1)} %get-tuple-element.20), channel_id=1, source_target_pairs={{0,1},{2,3},{4,5},{6,7},{8,9},{10,11},{12,13},{14,15},{16,17},{18,... | collective-permute-start | bytes 27656 | tf_op jit(solution)/shard_map/ppermute | solution.py:22
  222.5 3.1 %collective-permute-start.23 = (f32[18,1,128]{2,1,0:T(1,128)S(1)}, f32[18,1,128]{2,1,0:T(1,128)S(1)}, u32[]{:S(2)}, u32[]{:S(2)}) collective-permute-start(f32[18,1,128]{2,1,0:T(1,128)S(1)} %get-tuple-element.19), channel_id=1, source_target_pairs={{1,0},{3,2},{5,4},{7,6},{9,8},{11,10},{13,12},{15,14},{17,16},{19,... | collective-permute-start | bytes 27656 | tf_op jit(solution)/shard_map/ppermute | solution.py:24
  (2 other events, 64.3 us)
where the time goes:
time: 228 us; the launch traced here: 226 us
  blocking collectives  83.9 us (37%)
  starting transfers between devices  48.3 us (21%)
  waiting for transfers between devices  39 us (17%)
  other arithmetic  37.5 us (16%)
  local copies, waits for them, and re-layouts  13.4 us (6%)
  between operations  4.24 us (2%)
    unnamed x2, blocking collectives  83.9 us
    ppermute x10, starting transfers between devices, extended(): lax.ppermute(tail, axis, [(i, (i + 1) % count) for i in range(ends)])  30.3 us
    ppermute x10, waiting for transfers between devices, extended(): lax.ppermute(head, axis, [((i + 1) % count, i) for i in range(ends)])  24.9 us
    ppermute x10, starting transfers between devices, extended(): lax.ppermute(head, axis, [((i + 1) % count, i) for i in range(ends)])  12.9 us
    ppermute x4, waiting for transfers between devices, shifted(): return lax.ppermute(array, axis, pairs)  12.8 us
    unnamed x2, other arithmetic  5.32 us
    another operation x4, other arithmetic, body(): jnp.stack([jnp.stack([column_pair[0], north_pair[0]]), jnp.stack([column_...  5.27 us
    add x2, other arithmetic, interpolate(): corners[0, 0] * weights[0] + corners[1, 0] * weights[1]  5.14 us
  transfers between devices with their start and end apart: 24, of which 14 were waited for; matrix products, arithmetic and copies ran while one was open for 4% of the time, Pallas kernels for 0%

commit v1 on v0

v1 whole, which is shorter than its diff:
```python
import jax
import jax.numpy as jnp
from jax import lax
from jax.experimental import pallas as pl
from jax.experimental.pallas import tpu as pltpu
from jax.sharding import PartitionSpec as P

BLOCK = 8
SWEEPS = 4
ITERS = 2
reaction = 1.0
MESH = pl.DeviceIdType.MESH
SIDES = ((-1, 0), (1, 0), (0, -1), (0, 1))
SLOTS = [(a, b) for a in range(-1, 3) for b in range(-1, 3) if a in (0, 1) or b in (0, 1)]


def slot_at(a, b):
    return 4 * (a + 1) + (b + 1)


def make_kernel(wide, narrow, shape, blocks):
    cx, cy, nz = shape
    half = cx // 2
    count = wide * narrow
    blocks_x, blocks_y, blocks_z = blocks
    f32 = jnp.float32

    def kernel(
        rhs_hbm, labels_hbm, material, robin_table, robin_index, rows_hbm,
        sol_ref, res_ref,
        rhs, labels, labels_in, window, gathered, x_out, x_in, y_out, y_in, coef, diag_s,
        local_sem, label_send, label_recv, row_send, row_recv,
        face_send, face_recv, gather_send, gather_recv,
    ):
        w = lax.axis_index("wide")
        n = lax.axis_index("narrow")
        me = w * narrow + n
        loads = [
            pltpu.make_async_copy(labels_hbm, labels, local_sem.at[0]),
            pltpu.make_async_copy(rows_hbm, window.at[slot_at(0, 0)], local_sem.at[1]),
            pltpu.make_async_copy(rhs_hbm, rhs, local_sem.at[2]),
        ]
        labels_in[...] = jnp.zeros_like(labels_in)
        x_in[...] = jnp.zeros_like(x_in)
        y_in[...] = jnp.zeros_like(y_in)
        for a, b in SLOTS:
            if (a, b) != (0, 0):
                window[slot_at(a, b)] = jnp.zeros_like(window[slot_at(a, b)])
        for load in loads:
            load.start()
        barrier = pltpu.get_barrier_semaphore()

        def peer(step):
            flat = me + step
            flat = jnp.where(flat >= count, flat - count, flat)
            return (flat // narrow, flat % narrow)

        def greet(step, carry):
            pl.semaphore_signal(barrier, inc=1, device_id=peer(step), device_id_type=MESH)
            return carry

        lax.fori_loop(1, count, greet, 0)

        has = [w > 0, w < wide - 1, n > 0, n < narrow - 1]
        inside = [jnp.where(flag, 1.0, 0.0).astype(f32) for flag in has]
        p_x = robin_table[robin_index[0, 0, 0]]
        p_y = robin_table[robin_index[0, 0, 1]]

        spread = (
            lax.broadcasted_iota(jnp.int32, (blocks_z, nz), 1) // BLOCK
            == lax.broadcasted_iota(jnp.int32, (blocks_z, nz), 0)
        ).astype(f32)
        row_j = lax.broadcasted_iota(jnp.int32, (cy, nz), 0)
        lane_k = lax.broadcasted_iota(jnp.int32, (cy, nz), 1)
        even = (row_j + lane_k) % 2 == 0

        def kappa_rows(label_rows):
            wide_rows = jnp.dot(label_rows.astype(f32), spread, preferred_element_type=f32)
            found = jnp.zeros_like(wide_rows)
            for entry in range(material.shape[0]):
                found = jnp.where(wide_rows == float(entry), material[entry], found)
            return found

        def plane_of(rows):
            plane = jnp.broadcast_to(rows[blocks_y - 1 : blocks_y], (cy, nz))
            for at in range(blocks_y - 2, -1, -1):
                plane = jnp.where(row_j < (at + 1) * BLOCK, jnp.broadcast_to(rows[at : at + 1], (cy, nz)), plane)
            return plane

        loads[0].wait()
        loads[1].wait()
        kappa = [plane_of(kappa_rows(labels[bx])) for bx in range(blocks_x)]
        c_below, c_above = [], []
        for plane in kappa:
            c_below.append(0.5 * (plane + jnp.where(lane_k == 0, plane, pltpu.roll(plane, 1, 1))))
            c_above.append(0.5 * (plane + jnp.where(lane_k == nz - 1, plane, pltpu.roll(plane, nz - 1, 1))))

        pl.semaphore_wait(barrier, count - 1)

        def label_copy(side):
            dw, dn = SIDES[side]
            return pltpu.make_async_remote_copy(
                src_ref=labels, dst_ref=labels_in.at[side ^ 1],
                send_sem=label_send.at[side], recv_sem=label_recv.at[side ^ 1],
                device_id=(w + dw, n + dn), device_id_type=MESH,
            )

        def label_arrival(side):
            dw, dn = SIDES[side]
            return pltpu.make_async_remote_copy(
                src_ref=labels, dst_ref=labels_in.at[side],
                send_sem=label_send.at[side], recv_sem=label_recv.at[side],
                device_id=(w + dw, n + dn), device_id_type=MESH,
            )

        for side in range(4):
            @pl.when(has[side])
            def _(side=side):
                label_copy(side).start()

        def on_grid(a, b):
            return (w + a >= 0) & (w + a < wide) & (n + b >= 0) & (n + b < narrow)

        def row_copy(a, b):
            slot = slot_at(a, b)
            return pltpu.make_async_remote_copy(
                src_ref=window.at[slot_at(0, 0)], dst_ref=window.at[slot],
                send_sem=row_send.at[slot], recv_sem=row_recv.at[slot],
                device_id=(w - a, n - b), device_id_type=MESH,
            )

        far = [(a, b) for a, b in SLOTS if (a, b) != (0, 0) and abs(a) < wide and abs(b) < narrow]
        for a, b in far:
            @pl.when(on_grid(-a, -b))
            def _(a=a, b=b):
                row_copy(a, b).start()

        loads[2].wait()
        for side in range(4):
            @pl.when(has[side])
            def _(side=side):
                label_arrival(side).wait_recv()

        west_k = jnp.where(has[0], plane_of(kappa_rows(labels_in[0, blocks_x - 1])), kappa[0])
        east_k = jnp.where(has[1], plane_of(kappa_rows(labels_in[1, 0])), kappa[-1])
        c_south, c_north = [], []
        for bx in range(blocks_x):
            plane = kappa[bx]
            south_row = jnp.broadcast_to(kappa_rows(labels_in[2, bx])[blocks_y - 1 : blocks_y], (cy, nz))
            north_row = jnp.broadcast_to(kappa_rows(labels_in[3, bx])[0:1], (cy, nz))
            below = jnp.where(has[2], south_row, plane)
            above = jnp.where(has[3], north_row, plane)
            c_south.append(0.5 * (plane + jnp.where(row_j == 0, below, pltpu.roll(plane, 1, 0))))
            c_north.append(0.5 * (plane + jnp.where(row_j == cy - 1, above, pltpu.roll(plane, cy - 1, 0))))

        def x_face(i):
            left = west_k if i == 0 else kappa[(i - 1) // BLOCK]
            right = east_k if i == cx else kappa[i // BLOCK]
            return left if left is right else 0.5 * (left + right)

        faces = {}
        for i in range(cx + 1):
            key = (min(max(i - 1, -1), cx) // BLOCK, i // BLOCK)
            if key not in faces:
                faces[key] = x_face(i)
        c_x = [faces[((i - 1) // BLOCK if i else -1, i // BLOCK)] for i in range(cx + 1)]

        zero = jnp.zeros((cy, nz), f32)
        loc_south = [jnp.where(row_j == 0, 0.0, c) for c in c_south]
        loc_north = [jnp.where(row_j == cy - 1, 0.0, c) for c in c_north]
        loc_below = [jnp.where(lane_k == 0, 0.0, c) for c in c_below]
        loc_above = [jnp.where(lane_k == nz - 1, 0.0, c) for c in c_above]
        rob_y = p_y * (inside[2] * (row_j == 0).astype(f32) + inside[3] * (row_j == cy - 1).astype(f32))
        known = {}

        def plane_terms(i):
            bx = i // BLOCK
            key = (bx, i % BLOCK == 0, i % BLOCK == BLOCK - 1)
            if key not in known:
                total = reaction + c_x[i] + c_x[i + 1] + c_south[bx] + c_north[bx] + c_below[bx] + c_above[bx]
                local = total + rob_y
                if i == 0:
                    local = local + p_x * inside[0]
                if i == cx - 1:
                    local = local + p_x * inside[1]
                inv = 1.0 / local
                west = zero if i == 0 else c_x[i] * inv
                east = zero if i == cx - 1 else c_x[i + 1] * inv
                known[key] = (
                    total, inv, west, east, loc_south[bx] * inv, loc_north[bx] * inv,
                    loc_below[bx] * inv, loc_above[bx] * inv,
                )
            return known[key]

        for h in range(half):
            lo, hi = plane_terms(2 * h), plane_terms(2 * h + 1)
            diag_s[0, h] = lo[0]
            diag_s[1, h] = hi[0]
            for colour in range(2):
                low = even if colour == 0 else jnp.logical_not(even)
                coef[colour, 0, h] = jnp.where(low, lo[3], hi[2])
                coef[colour, 1, h] = jnp.where(low, lo[2], hi[3])
                for item in range(4):
                    coef[colour, 2 + item, h] = jnp.where(low, lo[4 + item], hi[4 + item])
                coef[colour, 6, h] = jnp.where(low, lo[1], hi[1])

        def stacked(planes):
            return jnp.stack(planes, 0)

        def by_block(planes, parity):
            return stacked([planes[(2 * h + parity) // BLOCK] for h in range(half)])

        even3 = jnp.broadcast_to(even[None], (half, cy, nz))

        def packed(pair):
            return jnp.where(even3, pair[0], pair[1]), jnp.where(even3, pair[1], pair[0])

        def up(v):
            return jnp.concatenate([v[1:], v[:1]], 0)

        def down(v):
            return jnp.concatenate([v[-1:], v[:-1]], 0)

        def coupling(other, colour):
            if colour == 0:
                across = jnp.where(even3, down(other), up(other))
            else:
                across = jnp.where(even3, up(other), down(other))
            total = coef[colour, 0] * other + coef[colour, 1] * across
            total = total + coef[colour, 2] * pltpu.roll(other, 1, 1)
            total = total + coef[colour, 3] * pltpu.roll(other, cy - 1, 1)
            total = total + coef[colour, 4] * pltpu.roll(other, 1, 2)
            return total + coef[colour, 5] * pltpu.roll(other, nz - 1, 2)

        def relax(red, black, source):
            scaled = packed(source)
            scaled = (scaled[0] * coef[0, 6], scaled[1] * coef[1, 6])
            for sweep in range(SWEEPS):
                red = scaled[0] if black is None else scaled[0] + coupling(black, 0)
                black = scaled[1] + coupling(red, 1)
            return red, black

        right = tuple(stacked([rhs[2 * h + parity] for h in range(half)]) for parity in range(2))

        def misfit(u):
            result = []
            for parity in range(2):
                mine, other = u[parity], u[1 - parity]
                faces_w = stacked([zero if 2 * h + parity == 0 else c_x[2 * h + parity] for h in range(half)])
                faces_e = stacked(
                    [zero if 2 * h + parity == cx - 1 else c_x[2 * h + parity + 1] for h in range(half)]
                )
                west = down(other) if parity == 0 else other
                east = other if parity == 0 else up(other)
                total = right[parity] - diag_s[parity] * mine + faces_w * west + faces_e * east
                total = total + by_block(loc_south, parity) * pltpu.roll(mine, 1, 1)
                total = total + by_block(loc_north, parity) * pltpu.roll(mine, cy - 1, 1)
                total = total + by_block(loc_below, parity) * pltpu.roll(mine, 1, 2)
                total = total + by_block(loc_above, parity) * pltpu.roll(mine, nz - 1, 2)
                result.append(total)
            return result

        xi = [(i + 0.5) / cx for i in range(cx)]
        eta = (row_j.astype(f32) + 0.5) / cy
        eta_first, eta_last = 0.5 / cy, (cy - 0.5) / cy

        def weigh_x(pair):
            lows, highs = None, None
            for i in range(cx):
                plane = pair[i % 2][i // 2]
                low, high = (1.0 - xi[i]) * plane, xi[i] * plane
                lows = low if lows is None else lows + low
                highs = high if highs is None else highs + high
            return lows, highs

        win_row = lax.broadcasted_iota(jnp.int32, (16, count), 0)
        win_lane = lax.broadcasted_iota(jnp.int32, (16, count), 1)
        point_w = w + win_row // 4 - 1
        point_n = n + win_row % 4 - 1
        point_ok = (point_w >= 0) & (point_w < wide) & (point_n >= 0) & (point_n < narrow)
        point = jnp.where(point_ok, point_w * narrow + point_n, -1)
        at_point = point == win_lane
        slot_row = lax.broadcasted_iota(jnp.int32, (16, nz), 0)

        def edge_coef(planes, parity, row):
            return stacked([planes[(2 * h + parity) // BLOCK][row : row + 1] for h in range(half)])

        south_c = [edge_coef(c_south, parity, 0) * inside[2] for parity in range(2)]
        north_c = [edge_coef(c_north, parity, cy - 1) * inside[3] for parity in range(2)]
        west_c = c_x[0] * inside[0]
        east_c = c_x[cx] * inside[1]

        def restrict(u):
            low, high = weigh_x(misfit(u))
            out_w = west_c * u[0][0]
            out_e = east_c * u[1][half - 1]
            sums = {
                -1: (1.0 - xi[-1]) * out_w,
                0: low + xi[-1] * out_w,
                1: high + (1.0 - xi[0]) * out_e,
                2: xi[0] * out_e,
            }
            out_s = weigh_x([south_c[parity] * u[parity][:, 0:1] for parity in range(2)])
            out_n = weigh_x([north_c[parity] * u[parity][:, cy - 1 : cy] for parity in range(2)])
            table = jnp.zeros((16, nz), f32)
            for a in range(-1, 3):
                near = jnp.sum(sums[a] * (1.0 - eta), 0, keepdims=True)
                away = jnp.sum(sums[a] * eta, 0, keepdims=True)
                entries = {0: near, 1: away}
                if a in (0, 1):
                    entries[-1] = (1.0 - eta_last) * out_s[a]
                    entries[0] = near + eta_last * out_s[a]
                    entries[1] = away + (1.0 - eta_first) * out_n[a]
                    entries[2] = eta_first * out_n[a]
                for b, entry in entries.items():
                    table = jnp.where(slot_row == slot_at(a, b), jnp.broadcast_to(entry, (16, nz)), table)
            summed = jnp.sum(table, 1, keepdims=True)
            return jnp.sum(jnp.where(at_point, summed, 0.0), 0, keepdims=True)

        def face_copy(turn, side):
            dw, dn = SIDES[side]
            if side < 2:
                source, target = x_out.at[turn, side], x_in.at[turn, side ^ 1]
            else:
                source, target = y_out.at[turn, side - 2], y_in.at[turn, (side ^ 1) - 2]
            return pltpu.make_async_remote_copy(
                src_ref=source, dst_ref=target,
                send_sem=face_send.at[turn, side], recv_sem=face_recv.at[turn, side ^ 1],
                device_id=(w + dw, n + dn), device_id_type=MESH,
            )

        def face_arrival(turn, side):
            dw, dn = SIDES[side]
            if side < 2:
                source, target = x_out.at[turn, side], x_in.at[turn, side]
            else:
                source, target = y_out.at[turn, side - 2], y_in.at[turn, side - 2]
            return pltpu.make_async_remote_copy(
                src_ref=source, dst_ref=target,
                send_sem=face_send.at[turn, side], recv_sem=face_recv.at[turn, side],
                device_id=(w + dw, n + dn), device_id_type=MESH,
            )

        def gather_all(turn):
            return pltpu.make_async_remote_copy(
                src_ref=gathered.at[turn, pl.ds(0, count - 1)], dst_ref=gathered.at[turn, pl.ds(0, count - 1)],
                send_sem=gather_send.at[turn], recv_sem=gather_recv.at[turn],
                device_id=peer(1), device_id_type=MESH,
            )

        red = black = None
        source = right
        for turn in range(ITERS):
            red, black = relax(red, black, source)
            u = [jnp.where(even3, red, black), jnp.where(even3, black, red)]
            x_out[turn, 0] = u[0][0]
            x_out[turn, 1] = u[1][half - 1]
            for parity in range(2):
                y_out[turn, 0, pl.ds(parity * half, half)] = u[parity][:, 0:1]
                y_out[turn, 1, pl.ds(parity * half, half)] = u[parity][:, cy - 1 : cy]
            for side in range(4):
                @pl.when(has[side])
                def _(turn=turn, side=side):
                    face_copy(turn, side).start()
            gathered[turn, me] = restrict(u)

            def scatter(step, carry, turn=turn):
                pltpu.make_async_remote_copy(
                    src_ref=gathered.at[turn, me], dst_ref=gathered.at[turn, me],
                    send_sem=gather_send.at[turn], recv_sem=gather_recv.at[turn],
                    device_id=peer(step), device_id_type=MESH,
                ).start()
                return carry

            lax.fori_loop(1, count, scatter, 0)
            for side in range(4):
                @pl.when(has[side])
                def _(turn=turn, side=side):
                    face_arrival(turn, side).wait_recv()
            if turn == 0:
                for a, b in far:
                    @pl.when(on_grid(a, b))
                    def _(a=a, b=b):
                        row_copy(a, b).wait_recv()
            gather_all(turn).wait_recv()
            load = jnp.sum(gathered[turn], 0)
            value = {}
            for a, b in SLOTS:
                value[a, b] = jnp.sum(window[slot_at(a, b)] * load, 1, keepdims=True)

            along = {a: value[a, 0] * (1.0 - eta) + value[a, 1] * eta for a in range(-1, 3)}
            u = [
                u[parity]
                + stacked(
                    [
                        (1.0 - xi[2 * h + parity]) * along[0] + xi[2 * h + parity] * along[1]
                        for h in range(half)
                    ]
                )
                for parity in range(2)
            ]
            west_u = x_in[turn, 0] + (1.0 - xi[-1]) * along[-1] + xi[-1] * along[0]
            east_u = x_in[turn, 1] + (1.0 - xi[0]) * along[1] + xi[0] * along[2]
            under = [value[a, -1] * (1.0 - eta_last) + value[a, 0] * eta_last for a in (0, 1)]
            over = [value[a, 1] * (1.0 - eta_first) + value[a, 2] * eta_first for a in (0, 1)]

            def edge(base, ends, parity):
                return base + stacked(
                    [
                        jnp.broadcast_to(
                            (1.0 - xi[2 * h + parity]) * ends[0] + xi[2 * h + parity] * ends[1], (1, nz)
                        )
                        for h in range(half)
                    ]
                )

            south_u = [edge(y_in[turn, 0, pl.ds(parity * half, half)], under, parity) for parity in range(2)]
            north_u = [edge(y_in[turn, 1, pl.ds(parity * half, half)], over, parity) for parity in range(2)]
            out_x = [west_c * west_u, east_c * east_u]
            out_y = [[south_c[parity] * south_u[parity] for parity in range(2)],
                     [north_c[parity] * north_u[parity] for parity in range(2)]]
            last = turn + 1 == ITERS
            if not last:
                out_x[0] = out_x[0] + (inside[0] * p_x) * u[0][0]
                out_x[1] = out_x[1] + (inside[1] * p_x) * u[1][half - 1]
                for parity in range(2):
                    out_y[0][parity] = out_y[0][parity] + (inside[2] * p_y) * u[parity][:, 0:1]
                    out_y[1][parity] = out_y[1][parity] + (inside[3] * p_y) * u[parity][:, cy - 1 : cy]
            base = misfit(u) if last else right
            row3 = jnp.broadcast_to(row_j[None], (half, cy, nz))
            total = []
            for parity in range(2):
                ends = jnp.where(row3 == 0, jnp.broadcast_to(out_y[0][parity], row3.shape), 0.0)
                ends = jnp.where(row3 == cy - 1, jnp.broadcast_to(out_y[1][parity], row3.shape), ends)
                total.append(base[parity] + ends)
            total[0] = jnp.concatenate([total[0][:1] + out_x[0][None], total[0][1:]], 0)
            total[1] = jnp.concatenate([total[1][:-1], total[1][-1:] + out_x[1][None]], 0)
            if last:
                for i in range(cx):
                    sol_ref[i] = u[i % 2][i // 2].astype(jnp.bfloat16)
                    res_ref[i] = total[i % 2][i // 2].astype(jnp.bfloat16)
            else:
                source = total
                red, black = packed(u)

        for side in range(4):
            @pl.when(has[side])
            def _(side=side):
                label_copy(side).wait_send()
                for turn in range(ITERS):
                    face_copy(turn, side).wait_send()
        for a, b in far:
            @pl.when(on_grid(-a, -b))
            def _(a=a, b=b):
                row_copy(a, b).wait_send()
        for turn in range(ITERS):
            gather_all(turn).wait_send()

    scratch = [
        pltpu.VMEM(shape, f32),
        pltpu.VMEM(blocks, jnp.int32),
        pltpu.VMEM((4,) + blocks, jnp.int32),
        pltpu.VMEM((16, 1, count), f32),
        pltpu.VMEM((ITERS, count, 1, count), f32),
        pltpu.VMEM((ITERS, 2, cy, nz), f32),
        pltpu.VMEM((ITERS, 2, cy, nz), f32),
        pltpu.VMEM((ITERS, 2, cx, 1, nz), f32),
        pltpu.VMEM((ITERS, 2, cx, 1, nz), f32),
        pltpu.VMEM((2, 7, half, cy, nz), f32),
        pltpu.VMEM((2, half, cy, nz), f32),
        pltpu.SemaphoreType.DMA((3,)),
        pltpu.SemaphoreType.DMA((4,)),
        pltpu.SemaphoreType.DMA((4,)),
        pltpu.SemaphoreType.DMA((16,)),
        pltpu.SemaphoreType.DMA((16,)),
        pltpu.SemaphoreType.DMA((ITERS, 4)),
        pltpu.SemaphoreType.DMA((ITERS, 4)),
        pltpu.SemaphoreType.DMA((ITERS,)),
        pltpu.SemaphoreType.DMA((ITERS,)),
    ]
    return kernel, scratch


def solution(mesh):
    wide, narrow = mesh.shape["wide"], mesh.shape["narrow"]

    def body(right_side, labels, material_table, robin_table, robin_index, coarse_rows):
        shape = right_side.shape
        kernel, scratch = make_kernel(wide, narrow, shape, labels.shape)
        anywhere = pl.BlockSpec(memory_space=pl.ANY)
        scalars = pl.BlockSpec(memory_space=pltpu.SMEM)
        vectors = pl.BlockSpec(memory_space=pltpu.VMEM)
        return pl.pallas_call(
            kernel,
            out_shape=(jax.ShapeDtypeStruct(shape, jnp.bfloat16),) * 2,
            in_specs=[anywhere, anywhere, scalars, scalars, scalars, anywhere],
            out_specs=(vectors, vectors),
            scratch_shapes=scratch,
            compiler_params=pltpu.CompilerParams(collective_id=0, has_side_effects=True),
        )(right_side, labels, material_table, robin_table, robin_index, coarse_rows)

    cells = P("wide", "narrow", None)
    return jax.shard_map(
        body,
        mesh=mesh,
        in_specs=(cells, cells, P(), P(), cells, P(("wide", "narrow"), None)),
        out_specs=(cells, cells),
        check_vma=False,
    )
```

time: 228 us -> 25.5 us (0.11)
  blocking collectives: 83.9 us -> 0 us
  starting transfers between devices: 48.3 us -> 0 us
  waiting for transfers between devices: 39 us -> 0 us
  other arithmetic: 37.5 us -> 0 us
  Pallas kernels: 0 us -> 22.5 us
  local copies, waits for them, and re-layouts: 13.4 us -> 2.14 us
  between operations: 4.24 us -> 0.65 us
    unnamed x2 -> x0, blocking collectives: 83.9 us -> none
    ppermute x24 -> x0, starting transfers between devices: 48.3 us -> none  [the longest x10 30.3 us: extended(): lax.ppermute(tail, axis, [(i, (i + 1) % count) for i in range(ends)])]
    ppermute x24 -> x0, waiting for transfers between devices: 39 us -> none  [the longest x10 24.9 us: extended(): lax.ppermute(head, axis, [((i + 1) % count, i) for i in range(ends)])]
    pallas_call x0 -> x1, Pallas kernels: none -> 22.5 us  [body(): pl.pallas_call(kernel, out_shape=(jax.ShapeDtypeStruct(shape, jnp.bfloat1...]
    slice x90 -> x0, local copies, waits for them, and re-layouts: 10 us -> none  [the longest x18 1.63 us: neighbour_sum(): field_now[:, :, :-1]]
    mul x4 -> x0, other arithmetic: 8.39 us -> none  [the longest x1 3.86 us: assemble_local(): robin_pair[1] * (inside[2] * marks[2] + inside[3] * marks[3])]
    another operation x6 -> x0, other arithmetic: 7.92 us -> none  [the longest x4 5.27 us: body(): jnp.stack([jnp.stack([column_pair[0], north_pair[0]]), jnp.stack([column_...]
    add x6 -> x0, other arithmetic: 5.47 us -> none  [the longest x2 5.14 us: interpolate(): corners[0, 0] * weights[0] + corners[1, 0] * weights[1]]
  transfers between devices with their start and end apart: 24 -> 0, of which waited for: 14 -> 0; matrix products, arithmetic and copies ran while one was open for 4% -> 0% of each run, Pallas kernels for 0% -> 0%
where the time goes in v1:
time: 25.5 us; the launch traced here: 25.3 us
  Pallas kernels  22.5 us (88%)
  local copies, waits for them, and re-layouts  2.14 us (8%)
  between operations  0.65 us (3%)
    pallas_call x1, Pallas kernels, body(): pl.pallas_call(kernel, out_shape=(jax.ShapeDtypeStruct(shape, jnp.bfloat1...  22.5 us
    unnamed x4, local copies, waits for them, and re-layouts  2.14 us

profile of v1, /device:TPU:0, one launch (start us, length us, event | category | flops | bytes accessed | tf_op | source)
XLA Modules:
  0.0 25.3 jit_solution(9452783436879259621)
XLA Ops:
  0.6 22.5 %shard_map.77 = (bf16[16,16,128]{2,1,0:T(8,128)(2,1)}, bf16[16,16,128]{2,1,0:T(8,128)(2,1)}) custom-call(f32[16,16,128]{2,1,0:T(8,128)} %rhs_hbm.1, s32[2,2,16]{2,1,0:T(2,128)} %labels_hbm.1, f32[16]{0:T(128)} %material.1, f32[8]{0:T(128)} %robin_table.1, s32[1,1,2]{2,1,0:T(1,128)} %robin_index.1, f32[1,32]{1,0:T(1,128)} %rows_hbm.1), custom_call_target="tpu_custom_call" | custom-call | tf_op jit(solution)/shard_map/pallas_call | solution.py:493
  23.2 0.0 copy-start
  23.2 1.5 %copy.10 = bf16[16,16,128]{2,1,0:T(8,128)(2,1)} copy(bf16[16,16,128]{2,1,0:T(8,128)(2,1)} %get-tuple-element.4) | data formatting | bytes 131072
  24.7 0.0 copy-done
  24.7 0.6 %copy.11 = bf16[16,16,128]{2,1,0:T(8,128)(2,1)} copy(bf16[16,16,128]{2,1,0:T(8,128)(2,1)S(1)} %copy-done) | data formatting | bytes 131072
Async XLA Ops:
  23.2 1.5 %copy-start = (bf16[16,16,128]{2,1,0:T(8,128)(2,1)S(1)}, bf16[16,16,128]{2,1,0:T(8,128)(2,1)}, u32[]{:S(2)}) copy-start(bf16[16,16,128]{2,1,0:T(8,128)(2,1)} %get-tuple-element.5) | copy-start | bytes 196612

commit v2 on v1

--- a/solution.py
+++ b/solution.py
@@ -22,19 +22,23 @@
     cx, cy, nz = shape
     half = cx // 2
     count = wide * narrow
+    low = 1
+    while low * low < wide or wide % low:
+        low += 1
+    high = wide // low
+    group = low * narrow
     blocks_x, blocks_y, blocks_z = blocks
     f32 = jnp.float32
 
     def kernel(
         rhs_hbm, labels_hbm, material, robin_table, robin_index, rows_hbm,
         sol_ref, res_ref,
-        rhs, labels, labels_in, window, gathered, x_out, x_in, y_out, y_in, coef, diag_s,
+        rhs, labels, labels_in, window, near_sums, far_sums, x_out, x_in, y_out, y_in, coef, diag_s,
         local_sem, label_send, label_recv, row_send, row_recv,
-        face_send, face_recv, gather_send, gather_recv,
+        face_send, face_recv, near_send, near_recv, far_send, far_recv,
     ):
         w = lax.axis_index("wide")
         n = lax.axis_index("narrow")
-        me = w * narrow + n
         loads = [
             pltpu.make_async_copy(labels_hbm, labels, local_sem.at[0]),
             pltpu.make_async_copy(rows_hbm, window.at[slot_at(0, 0)], local_sem.at[1]),
@@ -43,23 +47,41 @@
         labels_in[...] = jnp.zeros_like(labels_in)
         x_in[...] = jnp.zeros_like(x_in)
         y_in[...] = jnp.zeros_like(y_in)
-        for a, b in SLOTS:
-            if (a, b) != (0, 0):
-                window[slot_at(a, b)] = jnp.zeros_like(window[slot_at(a, b)])
+        for slot in range(16):
+            if slot != slot_at(0, 0):
+                window[slot] = jnp.zeros_like(window[slot])
         for load in loads:
             load.start()
         barrier = pltpu.get_barrier_semaphore()
 
-        def peer(step):
-            flat = me + step
-            flat = jnp.where(flat >= count, flat - count, flat)
-            return (flat // narrow, flat % narrow)
-
-        def greet(step, carry):
-            pl.semaphore_signal(barrier, inc=1, device_id=peer(step), device_id_type=MESH)
-            return carry
-
-        lax.fori_loop(1, count, greet, 0)
+        w_low, w_high = w % low, w // low
+
+        def near_peer(dw, dn):
+            return (w_high * low + (w_low + dw) % low, (n + dn) % narrow)
+
+        def far_peer(dw):
+            return ((w_high + dw) % high * low + w_low, n)
+
+        near = [(dw, dn) for dw in range(low) for dn in range(narrow)][:0:-1]
+        afar = list(range(1, high))
+        over_west = (w_low == 0) & (w > 0)
+        over_east = (w_low == low - 1) & (w < wide - 1)
+
+        def greet(target):
+            pl.semaphore_signal(barrier, inc=1, device_id=target, device_id_type=MESH)
+
+        @pl.when(over_west)
+        def _():
+            greet((w - 1, n))
+
+        @pl.when(over_east)
+        def _():
+            greet((w + 1, n))
+
+        for dw in afar:
+            greet(far_peer(dw))
+        for dw, dn in near:
+            greet(near_peer(dw, dn))
 
         has = [w > 0, w < wide - 1, n > 0, n < narrow - 1]
         inside = [jnp.where(flag, 1.0, 0.0).astype(f32) for flag in has]
@@ -95,7 +117,8 @@
             c_below.append(0.5 * (plane + jnp.where(lane_k == 0, plane, pltpu.roll(plane, 1, 1))))
             c_above.append(0.5 * (plane + jnp.where(lane_k == nz - 1, plane, pltpu.roll(plane, nz - 1, 1))))
 
-        pl.semaphore_wait(barrier, count - 1)
+        greeted = group + high - 2
+        pl.semaphore_wait(barrier, greeted + jnp.where(over_west, 1, 0) + jnp.where(over_east, 1, 0))
 
         def label_copy(side):
             dw, dn = SIDES[side]
@@ -118,31 +141,30 @@
             def _(side=side):
                 label_copy(side).start()
 
-        def on_grid(a, b):
-            return (w + a >= 0) & (w + a < wide) & (n + b >= 0) & (n + b < narrow)
-
-        def row_copy(a, b):
-            slot = slot_at(a, b)
-            return pltpu.make_async_remote_copy(
-                src_ref=window.at[slot_at(0, 0)], dst_ref=window.at[slot],
-                send_sem=row_send.at[slot], recv_sem=row_recv.at[slot],
-                device_id=(w - a, n - b), device_id_type=MESH,
-            )
-
-        far = [(a, b) for a, b in SLOTS if (a, b) != (0, 0) and abs(a) < wide and abs(b) < narrow]
-        for a, b in far:
-            @pl.when(on_grid(-a, -b))
-            def _(a=a, b=b):
-                row_copy(a, b).start()
-
-        loads[2].wait()
-        for side in range(4):
+        def row_step(kind, at, source, target, dw, dn):
+            return pltpu.make_async_remote_copy(
+                src_ref=source, dst_ref=target, send_sem=row_send.at[kind, at], recv_sem=row_recv.at[kind, at],
+                device_id=(w + dw, n + dn), device_id_type=MESH,
+            )
+
+        def column(a):
+            return window.at[pl.ds(4 * (a + 1), 4)]
+
+        own_row = window.at[slot_at(0, 0)]
+        row_south = row_step(0, 0, own_row, window.at[slot_at(0, 1)], 0, -1)
+        row_north = row_step(0, 1, own_row, window.at[slot_at(0, -1)], 0, 1)
+        row_again = row_step(1, 0, window.at[slot_at(0, 1)], window.at[slot_at(0, 2)], 0, -1)
+        column_west = row_step(2, 0, column(0), column(1), -1, 0)
+        column_east = row_step(2, 1, column(0), column(-1), 1, 0)
+        column_again = row_step(3, 0, column(1), column(2), -1, 0)
+        pl.when(has[2])(row_south.start)
+        pl.when(has[3])(row_north.start)
+
+        for side in (2, 3):
             @pl.when(has[side])
             def _(side=side):
                 label_arrival(side).wait_recv()
 
-        west_k = jnp.where(has[0], plane_of(kappa_rows(labels_in[0, blocks_x - 1])), kappa[0])
-        east_k = jnp.where(has[1], plane_of(kappa_rows(labels_in[1, 0])), kappa[-1])
         c_south, c_north = [], []
         for bx in range(blocks_x):
             plane = kappa[bx]
@@ -153,17 +175,11 @@
             c_south.append(0.5 * (plane + jnp.where(row_j == 0, below, pltpu.roll(plane, 1, 0))))
             c_north.append(0.5 * (plane + jnp.where(row_j == cy - 1, above, pltpu.roll(plane, cy - 1, 0))))
 
-        def x_face(i):
-            left = west_k if i == 0 else kappa[(i - 1) // BLOCK]
-            right = east_k if i == cx else kappa[i // BLOCK]
-            return left if left is right else 0.5 * (left + right)
-
-        faces = {}
-        for i in range(cx + 1):
-            key = (min(max(i - 1, -1), cx) // BLOCK, i // BLOCK)
-            if key not in faces:
-                faces[key] = x_face(i)
-        c_x = [faces[((i - 1) // BLOCK if i else -1, i // BLOCK)] for i in range(cx + 1)]
+        between = [0.5 * (kappa[bx] + kappa[bx + 1]) for bx in range(blocks_x - 1)]
+        c_x = [
+            kappa[i // BLOCK] if i % BLOCK else between[i // BLOCK - 1] if 0 < i < cx else None
+            for i in range(cx + 1)
+        ]
 
         zero = jnp.zeros((cy, nz), f32)
         loc_south = [jnp.where(row_j == 0, 0.0, c) for c in c_south]
@@ -192,7 +208,7 @@
                 )
             return known[key]
 
-        for h in range(half):
+        def set_planes(h):
             lo, hi = plane_terms(2 * h), plane_terms(2 * h + 1)
             diag_s[0, h] = lo[0]
             diag_s[1, h] = hi[0]
@@ -203,6 +219,28 @@
                 for item in range(4):
                     coef[colour, 2 + item, h] = jnp.where(low, lo[4 + item], hi[4 + item])
                 coef[colour, 6, h] = jnp.where(low, lo[1], hi[1])
+
+        for h in range(1, half - 1):
+            set_planes(h)
+        pl.when(has[3])(row_south.wait_recv)
+        pl.when(has[2])(row_north.wait_recv)
+        if narrow > 2:
+            pl.when(has[2] & has[3])(row_again.start)
+        for side in (0, 1):
+            @pl.when(has[side])
+            def _(side=side):
+                label_arrival(side).wait_recv()
+        west_k = jnp.where(has[0], plane_of(kappa_rows(labels_in[0, blocks_x - 1])), kappa[0])
+        east_k = jnp.where(has[1], plane_of(kappa_rows(labels_in[1, 0])), kappa[-1])
+        c_x[0] = 0.5 * (west_k + kappa[0])
+        c_x[cx] = 0.5 * (kappa[-1] + east_k)
+        set_planes(0)
+        set_planes(half - 1)
+        if narrow > 2:
+            pl.when(n + 2 < narrow)(row_again.wait_recv)
+        pl.when(has[0])(column_west.start)
+        pl.when(has[1])(column_east.start)
+        loads[2].wait()
 
         def stacked(planes):
             return jnp.stack(planes, 0)
@@ -341,12 +379,22 @@
                 device_id=(w + dw, n + dn), device_id_type=MESH,
             )
 
-        def gather_all(turn):
-            return pltpu.make_async_remote_copy(
-                src_ref=gathered.at[turn, pl.ds(0, count - 1)], dst_ref=gathered.at[turn, pl.ds(0, count - 1)],
-                send_sem=gather_send.at[turn], recv_sem=gather_recv.at[turn],
-                device_id=peer(1), device_id_type=MESH,
-            )
+        def spread_near(turn, dw, dn, rows):
+            return pltpu.make_async_remote_copy(
+                src_ref=near_sums.at[turn, rows], dst_ref=near_sums.at[turn, rows],
+                send_sem=near_send.at[turn], recv_sem=near_recv.at[turn],
+                device_id=near_peer(dw, dn), device_id_type=MESH,
+            )
+
+        def spread_far(turn, dw, rows):
+            return pltpu.make_async_remote_copy(
+                src_ref=far_sums.at[turn, rows], dst_ref=far_sums.at[turn, rows],
+                send_sem=far_send.at[turn], recv_sem=far_recv.at[turn],
+                device_id=far_peer(dw), device_id_type=MESH,
+            )
+
+        place = w_low * narrow + n
+        all_near, all_far = pl.ds(0, group - 1), pl.ds(0, high - 1)
 
         red = black = None
         source = right
@@ -362,28 +410,27 @@
                 @pl.when(has[side])
                 def _(turn=turn, side=side):
                     face_copy(turn, side).start()
-            gathered[turn, me] = restrict(u)
-
-            def scatter(step, carry, turn=turn):
-                pltpu.make_async_remote_copy(
-                    src_ref=gathered.at[turn, me], dst_ref=gathered.at[turn, me],
-                    send_sem=gather_send.at[turn], recv_sem=gather_recv.at[turn],
-                    device_id=peer(step), device_id_type=MESH,
-                ).start()
-                return carry
-
-            lax.fori_loop(1, count, scatter, 0)
+            near_sums[turn, place] = restrict(u)
+            for dw, dn in near:
+                spread_near(turn, dw, dn, place).start()
+            if turn == 0:
+                pl.when(has[1])(column_west.wait_recv)
+                pl.when(has[0])(column_east.wait_recv)
+                pl.when(has[0] & has[1])(column_again.start)
+            if near:
+                spread_near(turn, 0, 1, all_near).wait_recv()
+            far_sums[turn, w_high] = jnp.sum(near_sums[turn], 0)
+            for dw in afar:
+                spread_far(turn, dw, w_high).start()
             for side in range(4):
                 @pl.when(has[side])
                 def _(turn=turn, side=side):
                     face_arrival(turn, side).wait_recv()
             if turn == 0:
-                for a, b in far:
-                    @pl.when(on_grid(a, b))
-                    def _(a=a, b=b):
-                        row_copy(a, b).wait_recv()
-            gather_all(turn).wait_recv()
-            load = jnp.sum(gathered[turn], 0)
+                pl.when(w + 2 < wide)(column_again.wait_recv)
+            if afar:
+                spread_far(turn, 1, all_far).wait_recv()
+            load = jnp.sum(far_sums[turn], 0)
             value = {}
             for a, b in SLOTS:
                 value[a, b] = jnp.sum(window[slot_at(a, b)] * load, 1, keepdims=True)
@@ -449,19 +496,26 @@
                 label_copy(side).wait_send()
                 for turn in range(ITERS):
                     face_copy(turn, side).wait_send()
-        for a, b in far:
-            @pl.when(on_grid(-a, -b))
-            def _(a=a, b=b):
-                row_copy(a, b).wait_send()
+        pl.when(has[2])(row_south.wait_send)
+        pl.when(has[3])(row_north.wait_send)
+        if narrow > 2:
+            pl.when(has[2] & has[3])(row_again.wait_send)
+        pl.when(has[0])(column_west.wait_send)
+        pl.when(has[1])(column_east.wait_send)
+        pl.when(has[0] & has[1])(column_again.wait_send)
         for turn in range(ITERS):
-            gather_all(turn).wait_send()
+            if near:
+                spread_near(turn, 0, 1, all_near).wait_send()
+            if afar:
+                spread_far(turn, 1, all_far).wait_send()
 
     scratch = [
         pltpu.VMEM(shape, f32),
         pltpu.VMEM(blocks, jnp.int32),
         pltpu.VMEM((4,) + blocks, jnp.int32),
         pltpu.VMEM((16, 1, count), f32),
-        pltpu.VMEM((ITERS, count, 1, count), f32),
+        pltpu.VMEM((ITERS, group, 1, count), f32),
+        pltpu.VMEM((ITERS, high, 1, count), f32),
         pltpu.VMEM((ITERS, 2, cy, nz), f32),
         pltpu.VMEM((ITERS, 2, cy, nz), f32),
         pltpu.VMEM((ITERS, 2, cx, 1, nz), f32),
@@ -471,10 +525,12 @@
         pltpu.SemaphoreType.DMA((3,)),
         pltpu.SemaphoreType.DMA((4,)),
         pltpu.SemaphoreType.DMA((4,)),
-        pltpu.SemaphoreType.DMA((16,)),
-        pltpu.SemaphoreType.DMA((16,)),
+        pltpu.SemaphoreType.DMA((4, 2)),
+        pltpu.SemaphoreType.DMA((4, 2)),
         pltpu.SemaphoreType.DMA((ITERS, 4)),
         pltpu.SemaphoreType.DMA((ITERS, 4)),
+        pltpu.SemaphoreType.DMA((ITERS,)),
+        pltpu.SemaphoreType.DMA((ITERS,)),
         pltpu.SemaphoreType.DMA((ITERS,)),
         pltpu.SemaphoreType.DMA((ITERS,)),
     ]

time: 25.5 us -> 29.1 us (1.14)
  Pallas kernels: 22.5 us -> 26.2 us
    pallas_call x1, Pallas kernels: 22.5 us -> 26.2 us  [body(): pl.pallas_call(kernel, out_shape=(jax.ShapeDtypeStruct(shape, jnp.bfloat1...]
where the time goes in v2:
time: 29.1 us; the launch traced here: 28.9 us
  Pallas kernels  26.2 us (90%)
  local copies, waits for them, and re-layouts  2.14 us (7%)
  between operations  0.65 us (2%)
    pallas_call x1, Pallas kernels, body(): pl.pallas_call(kernel, out_shape=(jax.ShapeDtypeStruct(shape, jnp.bfloat1...  26.2 us
    unnamed x4, local copies, waits for them, and re-layouts  2.14 us

profile of v2, /device:TPU:0, one launch (start us, length us, event | category | flops | bytes accessed | tf_op | source)
XLA Modules:
  0.0 28.9 jit_solution(6994263721826670348)
XLA Ops:
  0.6 26.2 %shard_map.77 = (bf16[16,16,128]{2,1,0:T(8,128)(2,1)}, bf16[16,16,128]{2,1,0:T(8,128)(2,1)}) custom-call(f32[16,16,128]{2,1,0:T(8,128)} %rhs_hbm.1, s32[2,2,16]{2,1,0:T(2,128)} %labels_hbm.1, f32[16]{0:T(128)} %material.1, f32[8]{0:T(128)} %robin_table.1, s32[1,1,2]{2,1,0:T(1,128)} %robin_index.1, f32[1,32]{1,0:T(1,128)} %rows_hbm.1), custom_call_target="tpu_custom_call" | custom-call | tf_op jit(solution)/shard_map/pallas_call | solution.py:549
  26.8 0.0 copy-start
  26.8 1.5 %copy.10 = bf16[16,16,128]{2,1,0:T(8,128)(2,1)} copy(bf16[16,16,128]{2,1,0:T(8,128)(2,1)} %get-tuple-element.4) | data formatting | bytes 131072
  28.3 0.0 copy-done
  28.3 0.6 %copy.11 = bf16[16,16,128]{2,1,0:T(8,128)(2,1)} copy(bf16[16,16,128]{2,1,0:T(8,128)(2,1)S(1)} %copy-done) | data formatting | bytes 131072
Async XLA Ops:
  26.8 1.5 %copy-start = (bf16[16,16,128]{2,1,0:T(8,128)(2,1)S(1)}, bf16[16,16,128]{2,1,0:T(8,128)(2,1)}, u32[]{:S(2)}) copy-start(bf16[16,16,128]{2,1,0:T(8,128)(2,1)} %get-tuple-element.5) | copy-start | bytes 196612

commit v3 on v2

--- a/solution.py
+++ b/solution.py
@@ -18,24 +18,24 @@
     return 4 * (a + 1) + (b + 1)
 
 
-def make_kernel(wide, narrow, shape, blocks):
+def make_kernel(wide, narrow, shape, blocks, tables):
     cx, cy, nz = shape
     half = cx // 2
     count = wide * narrow
-    low = 1
-    while low * low < wide or wide % low:
-        low += 1
-    high = wide // low
-    group = low * narrow
+    paired = wide & (wide - 1) == 0 and narrow & (narrow - 1) == 0
+    bits = [(1 << k, 0) for k in reversed(range(wide.bit_length() - 1))]
+    bits += [(0, 1 << k) for k in range(narrow.bit_length() - 1)]
+    others = [(dw, dn) for dw in range(wide) for dn in range(narrow) if dw or dn]
+    others.sort(key=lambda by: (abs(by[0] - wide // 2), -by[1]))
     blocks_x, blocks_y, blocks_z = blocks
     f32 = jnp.float32
 
     def kernel(
-        rhs_hbm, labels_hbm, material, robin_table, robin_index, rows_hbm,
+        rhs_hbm, labels_hbm, material_hbm, robin_hbm, index_hbm, rows_hbm,
         sol_ref, res_ref,
-        rhs, labels, labels_in, window, near_sums, far_sums, x_out, x_in, y_out, y_in, coef, diag_s,
+        material, robin_table, robin_index, rhs, labels, labels_in, window, sums, x_out, x_in, y_out, y_in, coef, diag_s,
         local_sem, label_send, label_recv, row_send, row_recv,
-        face_send, face_recv, near_send, near_recv, far_send, far_recv,
+        face_send, face_recv, sum_send, sum_recv, known_sem,
     ):
         w = lax.axis_index("wide")
         n = lax.axis_index("narrow")
@@ -43,6 +43,9 @@
             pltpu.make_async_copy(labels_hbm, labels, local_sem.at[0]),
             pltpu.make_async_copy(rows_hbm, window.at[slot_at(0, 0)], local_sem.at[1]),
             pltpu.make_async_copy(rhs_hbm, rhs, local_sem.at[2]),
+            pltpu.make_async_copy(material_hbm, material, local_sem.at[3]),
+            pltpu.make_async_copy(robin_hbm, robin_table, local_sem.at[4]),
+            pltpu.make_async_copy(index_hbm, robin_index, local_sem.at[5]),
         ]
         labels_in[...] = jnp.zeros_like(labels_in)
         x_in[...] = jnp.zeros_like(x_in)
@@ -54,40 +57,44 @@
             load.start()
         barrier = pltpu.get_barrier_semaphore()
 
-        w_low, w_high = w % low, w // low
-
-        def near_peer(dw, dn):
-            return (w_high * low + (w_low + dw) % low, (n + dn) % narrow)
-
-        def far_peer(dw):
-            return ((w_high + dw) % high * low + w_low, n)
-
-        near = [(dw, dn) for dw in range(low) for dn in range(narrow)][:0:-1]
-        afar = list(range(1, high))
-        over_west = (w_low == 0) & (w > 0)
-        over_east = (w_low == low - 1) & (w < wide - 1)
-
-        def greet(target):
-            pl.semaphore_signal(barrier, inc=1, device_id=target, device_id_type=MESH)
-
-        @pl.when(over_west)
-        def _():
-            greet((w - 1, n))
-
-        @pl.when(over_east)
-        def _():
-            greet((w + 1, n))
-
-        for dw in afar:
-            greet(far_peer(dw))
-        for dw, dn in near:
-            greet(near_peer(dw, dn))
-
         has = [w > 0, w < wide - 1, n > 0, n < narrow - 1]
+        me = w * narrow + n
+
+        def flipped(at, bit):
+            return at + bit - 2 * bit * (at // bit % 2) if bit else at
+
+        def partner(stage):
+            return (flipped(w, bits[stage][0]), flipped(n, bits[stage][1]))
+
+        def signal(sem, target):
+            pl.semaphore_signal(sem, inc=1, device_id=target, device_id_type=MESH)
+
+        if paired:
+            for side in range(4):
+                @pl.when(has[side])
+                def _(side=side):
+                    signal(barrier, (w + SIDES[side][0], n + SIDES[side][1]))
+            greeted = sum(jnp.where(flag, 1, 0) for flag in has) + len(bits)
+            for stage in range(len(bits)):
+                signal(barrier, partner(stage))
+        else:
+            for dw, dn in others:
+                signal(barrier, ((w + dw) % wide, (n + dn) % narrow))
+            greeted = len(others)
+        stages = iter(range(len(bits)))
+
+        def begin_stage():
+            signal(known_sem.at[0], partner(0))
+
+        def next_stage():
+            stage = next(stages, None)
+            if paired and stage is not None:
+                pl.semaphore_wait(known_sem.at[stage], 1)
+                if stage + 1 < len(bits):
+                    signal(known_sem.at[stage + 1], partner(stage + 1))
+            return stage is not None
+
         inside = [jnp.where(flag, 1.0, 0.0).astype(f32) for flag in has]
-        p_x = robin_table[robin_index[0, 0, 0]]
-        p_y = robin_table[robin_index[0, 0, 1]]
-
         spread = (
             lax.broadcasted_iota(jnp.int32, (blocks_z, nz), 1) // BLOCK
             == lax.broadcasted_iota(jnp.int32, (blocks_z, nz), 0)
@@ -109,16 +116,18 @@
                 plane = jnp.where(row_j < (at + 1) * BLOCK, jnp.broadcast_to(rows[at : at + 1], (cy, nz)), plane)
             return plane
 
-        loads[0].wait()
-        loads[1].wait()
+        for at in (0, 1, 3, 4, 5):
+            loads[at].wait()
+        p_x = robin_table[robin_index[0, 0, 0]]
+        p_y = robin_table[robin_index[0, 0, 1]]
+
         kappa = [plane_of(kappa_rows(labels[bx])) for bx in range(blocks_x)]
         c_below, c_above = [], []
         for plane in kappa:
             c_below.append(0.5 * (plane + jnp.where(lane_k == 0, plane, pltpu.roll(plane, 1, 1))))
             c_above.append(0.5 * (plane + jnp.where(lane_k == nz - 1, plane, pltpu.roll(plane, nz - 1, 1))))
 
-        greeted = group + high - 2
-        pl.semaphore_wait(barrier, greeted + jnp.where(over_west, 1, 0) + jnp.where(over_east, 1, 0))
+        pl.semaphore_wait(barrier, greeted)
 
         def label_copy(side):
             dw, dn = SIDES[side]
@@ -160,10 +169,13 @@
         pl.when(has[2])(row_south.start)
         pl.when(has[3])(row_north.start)
 
+        if paired and bits:
+            begin_stage()
         for side in (2, 3):
             @pl.when(has[side])
             def _(side=side):
                 label_arrival(side).wait_recv()
+        next_stage()
 
         c_south, c_north = [], []
         for bx in range(blocks_x):
@@ -222,6 +234,7 @@
 
         for h in range(1, half - 1):
             set_planes(h)
+        next_stage()
         pl.when(has[3])(row_south.wait_recv)
         pl.when(has[2])(row_north.wait_recv)
         if narrow > 2:
@@ -230,6 +243,7 @@
             @pl.when(has[side])
             def _(side=side):
                 label_arrival(side).wait_recv()
+        next_stage()
         west_k = jnp.where(has[0], plane_of(kappa_rows(labels_in[0, blocks_x - 1])), kappa[0])
         east_k = jnp.where(has[1], plane_of(kappa_rows(labels_in[1, 0])), kappa[-1])
         c_x[0] = 0.5 * (west_k + kappa[0])
@@ -240,6 +254,7 @@
             pl.when(n + 2 < narrow)(row_again.wait_recv)
         pl.when(has[0])(column_west.start)
         pl.when(has[1])(column_east.start)
+        next_stage()
         loads[2].wait()
 
         def stacked(planes):
@@ -379,22 +394,14 @@
                 device_id=(w + dw, n + dn), device_id_type=MESH,
             )
 
-        def spread_near(turn, dw, dn, rows):
+        def spread_sum(turn, dw, dn, rows):
             return pltpu.make_async_remote_copy(
-                src_ref=near_sums.at[turn, rows], dst_ref=near_sums.at[turn, rows],
-                send_sem=near_send.at[turn], recv_sem=near_recv.at[turn],
-                device_id=near_peer(dw, dn), device_id_type=MESH,
+                src_ref=sums.at[turn, rows], dst_ref=sums.at[turn, rows],
+                send_sem=sum_send.at[turn], recv_sem=sum_recv.at[turn],
+                device_id=((w + dw) % wide, (n + dn) % narrow), device_id_type=MESH,
             )
 
-        def spread_far(turn, dw, rows):
-            return pltpu.make_async_remote_copy(
-                src_ref=far_sums.at[turn, rows], dst_ref=far_sums.at[turn, rows],
-                send_sem=far_send.at[turn], recv_sem=far_recv.at[turn],
-                device_id=far_peer(dw), device_id_type=MESH,
-            )
-
-        place = w_low * narrow + n
-        all_near, all_far = pl.ds(0, group - 1), pl.ds(0, high - 1)
+        received = pl.ds(0, count - 1)
 
         red = black = None
         source = right
@@ -410,27 +417,32 @@
                 @pl.when(has[side])
                 def _(turn=turn, side=side):
                     face_copy(turn, side).start()
-            near_sums[turn, place] = restrict(u)
-            for dw, dn in near:
-                spread_near(turn, dw, dn, place).start()
+            sums[turn, me] = restrict(u)
+            while next_stage():
+                pass
+            if count <= 64:
+                for dw, dn in others:
+                    spread_sum(turn, dw, dn, me).start()
+            else:
+                def scatter(step, carry, turn=turn):
+                    flat = (me + step) % count
+                    spread_sum(turn, flat // narrow + wide - w, flat % narrow + narrow - n, me).start()
+                    return carry
+
+                lax.fori_loop(1, count, scatter, 0)
             if turn == 0:
                 pl.when(has[1])(column_west.wait_recv)
                 pl.when(has[0])(column_east.wait_recv)
                 pl.when(has[0] & has[1])(column_again.start)
-            if near:
-                spread_near(turn, 0, 1, all_near).wait_recv()
-            far_sums[turn, w_high] = jnp.sum(near_sums[turn], 0)
-            for dw in afar:
-                spread_far(turn, dw, w_high).start()
             for side in range(4):
                 @pl.when(has[side])
                 def _(turn=turn, side=side):
                     face_arrival(turn, side).wait_recv()
             if turn == 0:
                 pl.when(w + 2 < wide)(column_again.wait_recv)
-            if afar:
-                spread_far(turn, 1, all_far).wait_recv()
-            load = jnp.sum(far_sums[turn], 0)
+            if others:
+                spread_sum(turn, *others[0], received).wait_recv()
+            load = jnp.sum(sums[turn], 0)
             value = {}
             for a, b in SLOTS:
                 value[a, b] = jnp.sum(window[slot_at(a, b)] * load, 1, keepdims=True)
@@ -504,25 +516,25 @@
         pl.when(has[1])(column_east.wait_send)
         pl.when(has[0] & has[1])(column_again.wait_send)
         for turn in range(ITERS):
-            if near:
-                spread_near(turn, 0, 1, all_near).wait_send()
-            if afar:
-                spread_far(turn, 1, all_far).wait_send()
+            if others:
+                spread_sum(turn, *others[0], received).wait_send()
 
     scratch = [
+        pltpu.SMEM(tables[0], f32),
+        pltpu.SMEM(tables[1], f32),
+        pltpu.SMEM(tables[2], jnp.int32),
         pltpu.VMEM(shape, f32),
         pltpu.VMEM(blocks, jnp.int32),
         pltpu.VMEM((4,) + blocks, jnp.int32),
         pltpu.VMEM((16, 1, count), f32),
-        pltpu.VMEM((ITERS, group, 1, count), f32),
-        pltpu.VMEM((ITERS, high, 1, count), f32),
+        pltpu.VMEM((ITERS, count, 1, count), f32),
         pltpu.VMEM((ITERS, 2, cy, nz), f32),
         pltpu.VMEM((ITERS, 2, cy, nz), f32),
         pltpu.VMEM((ITERS, 2, cx, 1, nz), f32),
         pltpu.VMEM((ITERS, 2, cx, 1, nz), f32),
         pltpu.VMEM((2, 7, half, cy, nz), f32),
         pltpu.VMEM((2, half, cy, nz), f32),
-        pltpu.SemaphoreType.DMA((3,)),
+        pltpu.SemaphoreType.DMA((6,)),
         pltpu.SemaphoreType.DMA((4,)),
         pltpu.SemaphoreType.DMA((4,)),
         pltpu.SemaphoreType.DMA((4, 2)),
@@ -531,8 +543,7 @@
         pltpu.SemaphoreType.DMA((ITERS, 4)),
         pltpu.SemaphoreType.DMA((ITERS,)),
         pltpu.SemaphoreType.DMA((ITERS,)),
-        pltpu.SemaphoreType.DMA((ITERS,)),
-        pltpu.SemaphoreType.DMA((ITERS,)),
+        pltpu.SemaphoreType.REGULAR((max(1, len(bits)),)),
     ]
     return kernel, scratch
 
@@ -542,14 +553,15 @@
 
     def body(right_side, labels, material_table, robin_table, robin_index, coarse_rows):
         shape = right_side.shape
-        kernel, scratch = make_kernel(wide, narrow, shape, labels.shape)
+        kernel, scratch = make_kernel(
+            wide, narrow, shape, labels.shape, (material_table.shape, robin_table.shape, robin_index.shape)
+        )
         anywhere = pl.BlockSpec(memory_space=pl.ANY)
-        scalars = pl.BlockSpec(memory_space=pltpu.SMEM)
         vectors = pl.BlockSpec(memory_space=pltpu.VMEM)
         return pl.pallas_call(
             kernel,
-            out_shape=(jax.ShapeDtypeStruct(shape, jnp.bfloat16),) * 2,
-            in_specs=[anywhere, anywhere, scalars, scalars, scalars, anywhere],
+            out_shape=(pltpu.VMEM(shape, jnp.bfloat16),) * 2,
+            in_specs=[anywhere] * 6,
             out_specs=(vectors, vectors),
             scratch_shapes=scratch,
             compiler_params=pltpu.CompilerParams(collective_id=0, has_side_effects=True),

time: 29.1 us -> 23.9 us (0.82)
  Pallas kernels: 26.2 us -> 21.8 us
  local copies, waits for them, and re-layouts: 2.14 us -> 1.26 us
    pallas_call x1, Pallas kernels: 26.2 us -> 21.8 us  [body(): pl.pallas_call(kernel, out_shape=(pltpu.VMEM(shape, jnp.bfloat16),) * 2,...]
    unnamed x4 -> x2, local copies, waits for them, and re-layouts: 2.14 us -> 1.26 us
where the time goes in v3:
time: 23.9 us; the launch traced here: 23.7 us
  Pallas kernels  21.8 us (91%)
  local copies, waits for them, and re-layouts  1.26 us (5%)
  between operations  0.64 us (3%)
    pallas_call x1, Pallas kernels, body(): pl.pallas_call(kernel, out_shape=(pltpu.VMEM(shape, jnp.bfloat16),) * 2,...  21.8 us
    unnamed x2, local copies, waits for them, and re-layouts  1.26 us

profile of v3, /device:TPU:0, one launch (start us, length us, event | category | flops | bytes accessed | tf_op | source)
XLA Modules:
  0.0 23.7 jit_solution(13162609878599597336)
XLA Ops:
  0.6 21.8 %shard_map.77 = (bf16[16,16,128]{2,1,0:T(8,128)(2,1)S(1)}, bf16[16,16,128]{2,1,0:T(8,128)(2,1)S(1)}) custom-call(f32[16,16,128]{2,1,0:T(8,128)} %rhs_hbm.1, s32[2,2,16]{2,1,0:T(2,128)} %labels_hbm.1, f32[16]{0:T(128)} %material_hbm.1, f32[8]{0:T(128)} %robin_hbm.1, s32[1,1,2]{2,1,0:T(1,128)} %index_hbm.1, f32[1,32]{1,0:T(1,128)} %rows_hbm.1), custom_call_target="tpu_custom_call" | custom-call | tf_op jit(solution)/shard_map/pallas_call | solution.py:561
  22.5 0.6 %copy.10 = bf16[16,16,128]{2,1,0:T(8,128)(2,1)} copy(bf16[16,16,128]{2,1,0:T(8,128)(2,1)S(1)} %get-tuple-element.2) | data formatting | bytes 131072
  23.1 0.6 %copy.11 = bf16[16,16,128]{2,1,0:T(8,128)(2,1)} copy(bf16[16,16,128]{2,1,0:T(8,128)(2,1)S(1)} %get-tuple-element.3) | data formatting | bytes 131072

commit v4 on v1

--- a/solution.py
+++ b/solution.py
@@ -18,19 +18,24 @@
     return 4 * (a + 1) + (b + 1)
 
 
-def make_kernel(wide, narrow, shape, blocks):
+def make_kernel(wide, narrow, shape, blocks, tables):
     cx, cy, nz = shape
     half = cx // 2
     count = wide * narrow
+    paired = wide & (wide - 1) == 0 and narrow & (narrow - 1) == 0
+    bits = [(1 << k, 0) for k in reversed(range(wide.bit_length() - 1))]
+    bits += [(0, 1 << k) for k in range(narrow.bit_length() - 1)]
+    others = [(dw, dn) for dw in range(wide) for dn in range(narrow) if dw or dn]
+    others.sort(key=lambda by: (abs(by[0] - wide // 2), -by[1]))
     blocks_x, blocks_y, blocks_z = blocks
     f32 = jnp.float32
 
     def kernel(
-        rhs_hbm, labels_hbm, material, robin_table, robin_index, rows_hbm,
+        rhs_hbm, labels_hbm, material_hbm, robin_hbm, index_hbm, rows_hbm,
         sol_ref, res_ref,
-        rhs, labels, labels_in, window, gathered, x_out, x_in, y_out, y_in, coef, diag_s,
+        material, robin_table, robin_index, rhs, labels, labels_in, window, gathered, x_out, x_in, y_out, y_in, coef, diag_s,
         local_sem, label_send, label_recv, row_send, row_recv,
-        face_send, face_recv, gather_send, gather_recv,
+        face_send, face_recv, gather_send, gather_recv, known_sem,
     ):
         w = lax.axis_index("wide")
         n = lax.axis_index("narrow")
@@ -39,6 +44,9 @@
             pltpu.make_async_copy(labels_hbm, labels, local_sem.at[0]),
             pltpu.make_async_copy(rows_hbm, window.at[slot_at(0, 0)], local_sem.at[1]),
             pltpu.make_async_copy(rhs_hbm, rhs, local_sem.at[2]),
+            pltpu.make_async_copy(material_hbm, material, local_sem.at[3]),
+            pltpu.make_async_copy(robin_hbm, robin_table, local_sem.at[4]),
+            pltpu.make_async_copy(index_hbm, robin_index, local_sem.at[5]),
         ]
         labels_in[...] = jnp.zeros_like(labels_in)
         x_in[...] = jnp.zeros_like(x_in)
@@ -55,17 +63,43 @@
             flat = jnp.where(flat >= count, flat - count, flat)
             return (flat // narrow, flat % narrow)
 
-        def greet(step, carry):
-            pl.semaphore_signal(barrier, inc=1, device_id=peer(step), device_id_type=MESH)
-            return carry
-
-        lax.fori_loop(1, count, greet, 0)
-
         has = [w > 0, w < wide - 1, n > 0, n < narrow - 1]
+
+        def flipped(at, bit):
+            return at + bit - 2 * bit * (at // bit % 2) if bit else at
+
+        def partner(stage):
+            return (flipped(w, bits[stage][0]), flipped(n, bits[stage][1]))
+
+        def signal(sem, target):
+            pl.semaphore_signal(sem, inc=1, device_id=target, device_id_type=MESH)
+
+        if paired:
+            for side in range(4):
+                @pl.when(has[side])
+                def _(side=side):
+                    signal(barrier, (w + SIDES[side][0], n + SIDES[side][1]))
+            greeted = sum(jnp.where(flag, 1, 0) for flag in has) + len(bits)
+            for stage in range(len(bits)):
+                signal(barrier, partner(stage))
+        else:
+            for dw, dn in others:
+                signal(barrier, ((w + dw) % wide, (n + dn) % narrow))
+            greeted = len(others)
+        stages = iter(range(len(bits)))
+
+        def begin_stage():
+            signal(known_sem.at[0], partner(0))
+
+        def next_stage():
+            stage = next(stages, None)
+            if paired and stage is not None:
+                pl.semaphore_wait(known_sem.at[stage], 1)
+                if stage + 1 < len(bits):
+                    signal(known_sem.at[stage + 1], partner(stage + 1))
+            return stage is not None
+
         inside = [jnp.where(flag, 1.0, 0.0).astype(f32) for flag in has]
-        p_x = robin_table[robin_index[0, 0, 0]]
-        p_y = robin_table[robin_index[0, 0, 1]]
-
         spread = (
             lax.broadcasted_iota(jnp.int32, (blocks_z, nz), 1) // BLOCK
             == lax.broadcasted_iota(jnp.int32, (blocks_z, nz), 0)
@@ -87,15 +121,18 @@
                 plane = jnp.where(row_j < (at + 1) * BLOCK, jnp.broadcast_to(rows[at : at + 1], (cy, nz)), plane)
             return plane
 
-        loads[0].wait()
-        loads[1].wait()
+        for at in (0, 1, 3, 4, 5):
+            loads[at].wait()
+        p_x = robin_table[robin_index[0, 0, 0]]
+        p_y = robin_table[robin_index[0, 0, 1]]
+
         kappa = [plane_of(kappa_rows(labels[bx])) for bx in range(blocks_x)]
         c_below, c_above = [], []
         for plane in kappa:
             c_below.append(0.5 * (plane + jnp.where(lane_k == 0, plane, pltpu.roll(plane, 1, 1))))
             c_above.append(0.5 * (plane + jnp.where(lane_k == nz - 1, plane, pltpu.roll(plane, nz - 1, 1))))
 
-        pl.semaphore_wait(barrier, count - 1)
+        pl.semaphore_wait(barrier, greeted)
 
         def label_copy(side):
             dw, dn = SIDES[side]
@@ -130,17 +167,17 @@
             )
 
         far = [(a, b) for a, b in SLOTS if (a, b) != (0, 0) and abs(a) < wide and abs(b) < narrow]
-        for a, b in far:
-            @pl.when(on_grid(-a, -b))
-            def _(a=a, b=b):
-                row_copy(a, b).start()
-
+        if paired and bits:
+            begin_stage()
+            next_stage()
+            next_stage()
         loads[2].wait()
         for side in range(4):
             @pl.when(has[side])
             def _(side=side):
                 label_arrival(side).wait_recv()
 
+        next_stage()
         west_k = jnp.where(has[0], plane_of(kappa_rows(labels_in[0, blocks_x - 1])), kappa[0])
         east_k = jnp.where(has[1], plane_of(kappa_rows(labels_in[1, 0])), kappa[-1])
         c_south, c_north = [], []
@@ -348,6 +385,7 @@
                 device_id=peer(1), device_id_type=MESH,
             )
 
+        next_stage()
         red = black = None
         source = right
         for turn in range(ITERS):
@@ -372,7 +410,14 @@
                 ).start()
                 return carry
 
+            while next_stage():
+                pass
             lax.fori_loop(1, count, scatter, 0)
+            if turn == 0:
+                for a, b in far:
+                    @pl.when(on_grid(-a, -b))
+                    def _(a=a, b=b):
+                        row_copy(a, b).start()
             for side in range(4):
                 @pl.when(has[side])
                 def _(turn=turn, side=side):
@@ -457,6 +502,9 @@
             gather_all(turn).wait_send()
 
     scratch = [
+        pltpu.SMEM(tables[0], f32),
+        pltpu.SMEM(tables[1], f32),
+        pltpu.SMEM(tables[2], jnp.int32),
         pltpu.VMEM(shape, f32),
         pltpu.VMEM(blocks, jnp.int32),
         pltpu.VMEM((4,) + blocks, jnp.int32),
@@ -468,7 +516,7 @@
         pltpu.VMEM((ITERS, 2, cx, 1, nz), f32),
         pltpu.VMEM((2, 7, half, cy, nz), f32),
         pltpu.VMEM((2, half, cy, nz), f32),
-        pltpu.SemaphoreType.DMA((3,)),
+        pltpu.SemaphoreType.DMA((6,)),
         pltpu.SemaphoreType.DMA((4,)),
         pltpu.SemaphoreType.DMA((4,)),
         pltpu.SemaphoreType.DMA((16,)),
@@ -477,6 +525,7 @@
         pltpu.SemaphoreType.DMA((ITERS, 4)),
         pltpu.SemaphoreType.DMA((ITERS,)),
         pltpu.SemaphoreType.DMA((ITERS,)),
+        pltpu.SemaphoreType.REGULAR((max(1, len(bits)),)),
     ]
     return kernel, scratch
 
@@ -486,14 +535,15 @@
 
     def body(right_side, labels, material_table, robin_table, robin_index, coarse_rows):
         shape = right_side.shape
-        kernel, scratch = make_kernel(wide, narrow, shape, labels.shape)
+        kernel, scratch = make_kernel(
+            wide, narrow, shape, labels.shape, (material_table.shape, robin_table.shape, robin_index.shape)
+        )
         anywhere = pl.BlockSpec(memory_space=pl.ANY)
-        scalars = pl.BlockSpec(memory_space=pltpu.SMEM)
         vectors = pl.BlockSpec(memory_space=pltpu.VMEM)
         return pl.pallas_call(
             kernel,
-            out_shape=(jax.ShapeDtypeStruct(shape, jnp.bfloat16),) * 2,
-            in_specs=[anywhere, anywhere, scalars, scalars, scalars, anywhere],
+            out_shape=(pltpu.VMEM(shape, jnp.bfloat16),) * 2,
+            in_specs=[anywhere] * 6,
             out_specs=(vectors, vectors),
             scratch_shapes=scratch,
             compiler_params=pltpu.CompilerParams(collective_id=0, has_side_effects=True),

time: 25.5 us -> 23.6 us (0.925)
  Pallas kernels: 22.5 us -> 21.6 us
  local copies, waits for them, and re-layouts: 2.14 us -> 1.26 us
    pallas_call x1, Pallas kernels: 22.5 us -> 21.6 us  [body(): pl.pallas_call(kernel, out_shape=(pltpu.VMEM(shape, jnp.bfloat16),) * 2,...]
    unnamed x4 -> x2, local copies, waits for them, and re-layouts: 2.14 us -> 1.26 us
where the time goes in v4:
time: 23.6 us; the launch traced here: 23.5 us
  Pallas kernels  21.6 us (92%)
  local copies, waits for them, and re-layouts  1.26 us (5%)
  between operations  0.64 us (3%)
    pallas_call x1, Pallas kernels, body(): pl.pallas_call(kernel, out_shape=(pltpu.VMEM(shape, jnp.bfloat16),) * 2,...  21.6 us
    unnamed x2, local copies, waits for them, and re-layouts  1.26 us

profile of v4, /device:TPU:0, one launch (start us, length us, event | category | flops | bytes accessed | tf_op | source)
XLA Modules:
  0.0 23.5 jit_solution(18436748984844207267)
XLA Ops:
  0.6 21.6 %shard_map.77 = (bf16[16,16,128]{2,1,0:T(8,128)(2,1)S(1)}, bf16[16,16,128]{2,1,0:T(8,128)(2,1)S(1)}) custom-call(f32[16,16,128]{2,1,0:T(8,128)} %rhs_hbm.1, s32[2,2,16]{2,1,0:T(2,128)} %labels_hbm.1, f32[16]{0:T(128)} %material_hbm.1, f32[8]{0:T(128)} %robin_hbm.1, s32[1,1,2]{2,1,0:T(1,128)} %index_hbm.1, f32[1,32]{1,0:T(1,128)} %rows_hbm.1), custom_call_target="tpu_custom_call" | custom-call | tf_op jit(solution)/shard_map/pallas_call | solution.py:543
  22.2 0.6 %copy.10 = bf16[16,16,128]{2,1,0:T(8,128)(2,1)} copy(bf16[16,16,128]{2,1,0:T(8,128)(2,1)S(1)} %get-tuple-element.2) | data formatting | bytes 131072
  22.8 0.6 %copy.11 = bf16[16,16,128]{2,1,0:T(8,128)(2,1)} copy(bf16[16,16,128]{2,1,0:T(8,128)(2,1)S(1)} %get-tuple-element.3) | data formatting | bytes 131072

commit v5 on v4

--- a/solution.py
+++ b/solution.py
@@ -22,7 +22,7 @@
     cx, cy, nz = shape
     half = cx // 2
     count = wide * narrow
-    paired = wide & (wide - 1) == 0 and narrow & (narrow - 1) == 0
+    paired = False
     bits = [(1 << k, 0) for k in reversed(range(wide.bit_length() - 1))]
     bits += [(0, 1 << k) for k in range(narrow.bit_length() - 1)]
     others = [(dw, dn) for dw in range(wide) for dn in range(narrow) if dw or dn]
@@ -167,6 +167,11 @@
             )
 
         far = [(a, b) for a, b in SLOTS if (a, b) != (0, 0) and abs(a) < wide and abs(b) < narrow]
+        for a, b in far:
+            @pl.when(on_grid(-a, -b))
+            def _(a=a, b=b):
+                row_copy(a, b).start()
+
         if paired and bits:
             begin_stage()
             next_stage()
@@ -412,12 +417,7 @@
 
             while next_stage():
                 pass
-            lax.fori_loop(1, count, scatter, 0)
-            if turn == 0:
-                for a, b in far:
-                    @pl.when(on_grid(-a, -b))
-                    def _(a=a, b=b):
-                        row_copy(a, b).start()
+            lax.fori_loop(1, count, scatter, 0, unroll=count <= 64)
             for side in range(4):
                 @pl.when(has[side])
                 def _(turn=turn, side=side):

time: 23.6 us -> 23.2 us (0.983)
  Pallas kernels: 21.6 us -> 21.1 us
    pallas_call x1, Pallas kernels: 21.6 us -> 21.1 us  [body(): pl.pallas_call(kernel, out_shape=(pltpu.VMEM(shape, jnp.bfloat16),) * 2,...]
where the time goes in v5:
time: 23.2 us; the launch traced here: 23.1 us
  Pallas kernels  21.1 us (91%)
  local copies, waits for them, and re-layouts  1.26 us (5%)
  between operations  0.64 us (3%)
    pallas_call x1, Pallas kernels, body(): pl.pallas_call(kernel, out_shape=(pltpu.VMEM(shape, jnp.bfloat16),) * 2,...  21.1 us
    unnamed x2, local copies, waits for them, and re-layouts  1.26 us

profile of v5, /device:TPU:0, one launch (start us, length us, event | category | flops | bytes accessed | tf_op | source)
XLA Modules:
  0.0 23.1 jit_solution(11650390376810335109)
XLA Ops:
  0.6 21.1 %shard_map.77 = (bf16[16,16,128]{2,1,0:T(8,128)(2,1)S(1)}, bf16[16,16,128]{2,1,0:T(8,128)(2,1)S(1)}) custom-call(f32[16,16,128]{2,1,0:T(8,128)} %rhs_hbm.1, s32[2,2,16]{2,1,0:T(2,128)} %labels_hbm.1, f32[16]{0:T(128)} %material_hbm.1, f32[8]{0:T(128)} %robin_hbm.1, s32[1,1,2]{2,1,0:T(1,128)} %index_hbm.1, f32[1,32]{1,0:T(1,128)} %rows_hbm.1), custom_call_target="tpu_custom_call" | custom-call | tf_op jit(solution)/shard_map/pallas_call | solution.py:543
  21.8 0.6 %copy.10 = bf16[16,16,128]{2,1,0:T(8,128)(2,1)} copy(bf16[16,16,128]{2,1,0:T(8,128)(2,1)S(1)} %get-tuple-element.2) | data formatting | bytes 131072
  22.4 0.6 %copy.11 = bf16[16,16,128]{2,1,0:T(8,128)(2,1)} copy(bf16[16,16,128]{2,1,0:T(8,128)(2,1)S(1)} %get-tuple-element.3) | data formatting | bytes 131072
